TPU v7x, 512 devices: a whole 4x4x16 slice. The times are simulated.
512 devices in a mesh: seq: 16 (over z), head: 16 (over y, x), dp: 2 (over core).
Axes of the slice: x: 4, y: 4, z: 16, core: 2. Of those that a mesh axis runs over, the one named last changes fastest.
Arguments:
- local_qkv: bfloat16 [3, 32768, 2048], P(None, ('dp', 'seq'), 'head'), parts along dimension 1, may hold values from -150 to 150
- local_grad: bfloat16 [32768, 2048], P(('dp', 'seq'), 'head'), parts along dimension 0, may hold values from -5 to 5
- routed_qkv: bfloat16 [3, 32768, 2048], P(None, ('dp', 'seq'), 'head'), parts along dimension 1, may hold values from -150 to 150
- routed_grad: bfloat16 [32768, 2048], P(('dp', 'seq'), 'head'), parts along dimension 0, may hold values from -5 to 5
- cluster_ids: int32 [16, 32768], P('head', ('dp', 'seq')), parts along dimension 1, may hold values from 0 to 15, as said below
Outputs:
- local_out: bfloat16 [32768, 2048], P(('dp', 'seq'), 'head'), parts along dimension 0
- local_dqkv: bfloat16 [3, 32768, 2048], P(None, ('dp', 'seq'), 'head'), parts along dimension 1
- routed_out: bfloat16 [32768, 2048], P(('dp', 'seq'), 'head'), parts along dimension 0
- routed_dqkv: bfloat16 [3, 32768, 2048], P(None, ('dp', 'seq'), 'head'), parts along dimension 1
There are 2 independent parts, one for each index of `dp`. A program takes and returns all parts, laid end to end along the dimension named above; each array names one. Nothing has to cross between parts.
Inputs may be any that keep to these rules, and one draw needn't show every extreme that they name: `cluster_ids`: for every clustered head each cluster holds exactly 1024 tokens, and at most 96 of the 1024 tokens of one index of seq lie in one cluster; some cluster reaches 96 in some index of seq.
All inputs are finite; a program needn't handle non-finite values.
Results may differ from a plain program's by a relative error of at most 0.024.
Values may be sent and summed in bfloat16 or wider, within the bound.
No kernel may reach another device: no remote copies, remote signals or barrier semaphores. Data moves between devices by JAX's collectives and lax.ppermute only.
A program may use at most 64 MiB of HBM per device.

v0:
```python
import jax
import jax.numpy as jnp
from jax import lax
from jax.sharding import PartitionSpec as P

WIN = 1024
CL_DEV = 1


masked_fill = -1e30


def shifted(block, axis, distance):
    devices = range(lax.axis_size(axis))
    route = [(i - distance, i) for i in devices if i - distance in devices]
    return lax.ppermute(block, axis, route)


def attend_rows(query_rows, grad_rows, key_rows, value_rows, allowed):
    factor = query_rows.shape[-1] ** (-0.5)
    scores = (
        jnp.einsum("qd,kd->qk", query_rows, key_rows, preferred_element_type=jnp.float32) * factor
    )
    scores = jnp.where(allowed, scores, masked_fill)
    row_peak = jnp.max(scores, axis=1, keepdims=True)
    exp_scores = jnp.exp(scores - row_peak)
    row_total = jnp.sum(exp_scores, axis=1, keepdims=True)
    row_probs = exp_scores / row_total
    weights = row_probs.astype(jnp.bfloat16)
    output = jnp.dot(weights, value_rows, preferred_element_type=jnp.float32).astype(jnp.bfloat16)
    output = lax.optimization_barrier(output)
    row_delta = jnp.sum(grad_rows.astype(jnp.float32) * output.astype(jnp.float32), axis=1)
    dprobs = jnp.einsum("qd,kd->qk", grad_rows, value_rows, preferred_element_type=jnp.float32)
    dscore = (row_probs * (dprobs - row_delta[:, None])).astype(jnp.bfloat16)
    dquery = (jnp.dot(dscore, key_rows, preferred_element_type=jnp.float32) * factor).astype(
        jnp.bfloat16
    )
    log_total = row_peak[:, 0] + jnp.log(row_total[:, 0])
    return (output, dquery, dscore, weights, log_total, row_delta)


def key_terms(dscore, weights, query_rows, grad_rows):
    factor = query_rows.shape[-1] ** (-0.5)
    key_grad = (
        jnp.einsum("qk,qd->kd", dscore, query_rows, preferred_element_type=jnp.float32) * factor
    )
    dvalue = jnp.einsum("qk,qd->kd", weights, grad_rows, preferred_element_type=jnp.float32)
    return (key_grad, dvalue)


def place_rows(term, start, total):
    return jnp.pad(term, ((start, total - start - term.shape[0]), (0, 0)))


def cluster_pass(packed, present_rows):
    member_count = packed.shape[0]
    head_size = packed.shape[-1]
    query_block = 512
    block_total = member_count // query_block
    key_rows = packed[:, 1]
    value_rows = packed[:, 2]
    allowed = jnp.broadcast_to(present_rows[None, :] > 0, (query_block, member_count))
    query_blocks = packed[:, 0].reshape(block_total, query_block, head_size)
    grad_blocks = packed[:, 3].reshape(block_total, query_block, head_size)

    def block_step(carried, rows):
        key_acc, value_acc = carried
        query_part, grad_part = rows
        output, dquery, dscore, weights, log_total, row_delta = attend_rows(
            query_part, grad_part, key_rows, value_rows, allowed
        )
        key_grad, dvalue = key_terms(dscore, weights, query_part, grad_part)
        return ((key_acc + key_grad, value_acc + dvalue), (output, dquery))

    initial = (
        jnp.zeros((member_count, head_size), jnp.float32),
        jnp.zeros((member_count, head_size), jnp.float32),
    )
    (key_acc, value_acc), (outputs, dqueries) = lax.scan(
        block_step, initial, (query_blocks, grad_blocks)
    )
    output = outputs.reshape(member_count, head_size)
    dquery = dqueries.reshape(member_count, head_size)
    return jnp.stack(
        [output, dquery, key_acc.astype(jnp.bfloat16), value_acc.astype(jnp.bfloat16)], axis=1
    )


def owner_work(received):
    payload, present = received
    sources, item_count, slot_cap = present.shape
    head_size = payload.shape[-1]
    gathered = jnp.transpose(payload, (1, 0, 2, 3, 4)).reshape(
        item_count, sources * slot_cap, 4, head_size
    )
    present_rows = jnp.transpose(present, (1, 0, 2)).reshape(item_count, sources * slot_cap)
    results = jax.vmap(cluster_pass)(gathered, present_rows)
    arranged = jnp.transpose(
        results.reshape(item_count, sources, slot_cap, 4, head_size), (1, 0, 2, 3, 4)
    )
    return lax.all_to_all(arranged, "seq", split_axis=0, concat_axis=0, tiled=True)


def cluster_ranks(labels, clusters, tok_rows):
    rank_block = min(tok_rows, 512)
    block_total = tok_rows // rank_block
    cluster_index = jnp.arange(clusters, dtype=jnp.int32)
    onehot = (
        (labels[:, None] == cluster_index[None, :])
        .astype(jnp.bfloat16)
        .reshape(block_total, rank_block, clusters)
    )
    spots = jnp.arange(rank_block, dtype=jnp.int32)
    lower = (spots[:, None] >= spots[None, :]).astype(jnp.bfloat16)

    def rank_step(running, block_onehot):
        within = jnp.dot(lower, block_onehot, preferred_element_type=jnp.float32) + running[None, :]
        ranks = jnp.sum(within * block_onehot.astype(jnp.float32), axis=1)
        return (running + jnp.sum(block_onehot.astype(jnp.float32), axis=0), ranks)

    unused, ranks = lax.scan(rank_step, jnp.zeros((clusters,), jnp.float32), onehot)
    return ranks.reshape(tok_rows).astype(jnp.int32) - 1


def on_device(local_qkv, local_grad, routed_qkv, routed_grad, cluster_ids):
    tok_rows = local_qkv.shape[1]
    head_size = local_qkv.shape[2]
    block_rows = min(tok_rows, 512)
    key_span = WIN + block_rows
    block_count = tok_rows // block_rows
    query_rows = local_qkv[0]
    key_rows = local_qkv[1]
    value_rows = local_qkv[2]
    prev_keys, prev_values = shifted((key_rows, value_rows), "seq", 1)
    joined_keys = jnp.concatenate([prev_keys, key_rows], axis=0)
    joined_values = jnp.concatenate([prev_values, value_rows], axis=0)
    anchor = lax.axis_index("seq") * tok_rows
    outputs, dqueries, totals, deltas = ([], [], [], [])
    key_acc = jnp.zeros((2 * tok_rows, head_size), jnp.float32)
    value_acc = jnp.zeros((2 * tok_rows, head_size), jnp.float32)
    for block_index in range(block_count):
        row_start = block_index * block_rows
        key_lower = tok_rows + row_start - WIN
        relative = key_lower - tok_rows + jnp.arange(key_span, dtype=jnp.int32)
        query_pos = row_start + jnp.arange(block_rows, dtype=jnp.int32)
        allowed = (
            (relative[None, :] <= query_pos[:, None])
            & (relative[None, :] > query_pos[:, None] - WIN)
            & (anchor + relative >= 0)[None, :]
        )
        query_block = query_rows[row_start : row_start + block_rows]
        grad_block = local_grad[row_start : row_start + block_rows]
        output, dquery, dscore, weights, log_total, row_delta = attend_rows(
            query_block,
            grad_block,
            joined_keys[key_lower : key_lower + key_span],
            joined_values[key_lower : key_lower + key_span],
            allowed,
        )
        outputs.append(output)
        dqueries.append(dquery)
        totals.append(log_total)
        deltas.append(row_delta)
        key_grad, dvalue = key_terms(dscore, weights, query_block, grad_block)
        key_acc = key_acc + place_rows(key_grad, key_lower, 2 * tok_rows)
        value_acc = value_acc + place_rows(dvalue, key_lower, 2 * tok_rows)
    late_keys, late_values = shifted((key_acc[:tok_rows], value_acc[:tok_rows]), "seq", -1)
    key_final = (key_acc[tok_rows:] + late_keys).astype(jnp.bfloat16)
    value_final = (value_acc[tok_rows:] + late_values).astype(jnp.bfloat16)
    local_out = jnp.concatenate(outputs, axis=0)
    local_dqkv = jnp.stack([jnp.concatenate(dqueries, axis=0), key_final, value_final])
    labels = cluster_ids[0]
    seq_count = lax.axis_size("seq")
    per_owner = CL_DEV
    clusters = per_owner * seq_count
    slot_cap = 3 * (tok_rows // per_owner) // (2 * seq_count)
    slot_rank = cluster_ranks(labels, clusters, tok_rows)
    target = labels * slot_cap + slot_rank
    slot_index = jnp.arange(clusters * slot_cap, dtype=jnp.int32)
    token_index = jnp.arange(tok_rows, dtype=jnp.int32)
    matches = target[None, :] == slot_index[:, None]
    source = jnp.sum(jnp.where(matches, token_index[None, :], 0), axis=1)
    filled = jnp.any(matches, axis=1)
    payload = jnp.stack([routed_qkv[0], routed_qkv[1], routed_qkv[2], routed_grad], axis=1)
    buffer = jnp.where(filled[:, None, None], payload[source], jnp.zeros((), jnp.bfloat16))
    present = filled.astype(jnp.bfloat16)
    returned = owner_work(
        (
            lax.all_to_all(
                buffer.reshape(seq_count, per_owner, slot_cap, 4, head_size),
                "seq",
                split_axis=0,
                concat_axis=0,
                tiled=True,
            ),
            lax.all_to_all(
                present.reshape(seq_count, per_owner, slot_cap),
                "seq",
                split_axis=0,
                concat_axis=0,
                tiled=True,
            ),
        )
    )
    returned = returned.reshape(clusters * slot_cap, 4, head_size)[target]
    routed_out = returned[:, 0]
    routed_dqkv = jnp.transpose(returned[:, 1:], (1, 0, 2))
    return (local_out, local_dqkv, routed_out, routed_dqkv)


def solution(mesh):
    placed = (
        P(None, ("dp", "seq"), "head"),
        P(("dp", "seq"), "head"),
        P(None, ("dp", "seq"), "head"),
        P(("dp", "seq"), "head"),
        P("head", ("dp", "seq")),
    )
    return jax.shard_map(
        on_device,
        mesh=mesh,
        in_specs=placed,
        out_specs=(
            P(("dp", "seq"), "head"),
            P(None, ("dp", "seq"), "head"),
            P(("dp", "seq"), "head"),
            P(None, ("dp", "seq"), "head"),
        ),
        check_vma=False,
    )
```

profile of v0, /device:TPU:24, one launch (start us, length us, event | category | flops | bytes accessed | tf_op | source)
XLA Modules:
  0.0 288.1 jit_solution(17753291535403448453)
XLA Ops:
  1.2 1.3 reduce.12
  2.6 0.9 while.30
  3.5 0.7 multiply_add_fusion
  4.2 0.8 fusion.43
  5.0 0.7 reshape.283
  5.7 15.2 %all-to-all-start = ((bf16[16,1,96]{2,1,0:T(2,128)(2,1)}), bf16[16,1,96]{2,1,0:T(2,128)(2,1)S(1)}, u32[]{:S(2)}, u32[]{:S(2)}) async-start(bf16[16,1,96]{2,1,0:T(2,128)(2,1)} %reshape.283), calls=%async_computation | async-start | bytes 16384 | tf_op jit(solution)/shard_map/all_to_all | solution.py:196
  20.9 0.7 select_reduce_fusion
  21.7 1.4 copy.48
  24.4 2.4 pad_maximum_fusion.1
  26.9 5.1 %gather_fusion = bf16[1536,4,128]{2,1,0:T(4,128)(2,1)S(1)} fusion(bf16[1024,4,128]{2,1,0:T(4,128)(2,1)S(1)} %pad_maximum_fusion.1, s32[2048]{0:T(1024)S(1)} %pad_clamp_fusion), kind=kCustom, calls=%fused_computation | custom fusion | bytes 3151872 | tf_op jit(solution)/shard_map/gather | solution.py:185
  32.0 4.1 %broadcast_select_fusion.1 = bf16[16,1,96,4,128]{4,3,2,1,0:T(4,128)(2,1)} fusion(bf16[16,1,96,4,128]{4,3,2,1,0:T(4,128)(2,1)S(1)} %bitcast.195, pred[16,96]{1,0:T(8,128)(4,1)S(1)} %broadcast_in_dim.53), kind=kLoop, calls=%fused_computation.84 | loop fusion | flops 786432 | bytes 3147264 | tf_op jit(solution)/shard_map/jit(_where)/select_n | solution.py:185
  36.1 12.0 %all-to-all-start.1 = ((bf16[16,1,96,4,128]{4,3,2,1,0:T(4,128)(2,1)}), bf16[16,1,96,4,128]{4,3,2,1,0:T(4,128)(2,1)S(1)}, u32[]{:S(2)}, u32[]{:S(2)}) async-start(bf16[16,1,96,4,128]{4,3,2,1,0:T(4,128)(2,1)} %broadcast_select_fusion.1), calls=%async_computation.1 | async-start | bytes 3145728 | tf_op jit(solution)/shard_map/all_to_all | solution.py:189
  48.2 0.7 slice_bitcast_fusion.6
  48.9 3.8 %collective-permute-start = (bf16[1024,128]{1,0:T(8,128)(2,1)S(1)}, bf16[1024,128]{1,0:T(8,128)(2,1)S(1)}, u32[]{:S(2)}, u32[]{:S(2)}) collective-permute-start(bf16[1024,128]{1,0:T(8,128)(2,1)S(1)} %get-tuple-element.226), channel_id=1, source_target_pairs={{0,32},{32,64},{64,96},{96,128},{128,160},{160,192},{192,224},{224... | collective-permute-start | bytes 786440 | tf_op jit(solution)/shard_map/ppermute | solution.py:16
  52.8 4.1 %collective-permute-start.1 = (bf16[1024,128]{1,0:T(8,128)(2,1)}, bf16[1024,128]{1,0:T(8,128)(2,1)}, u32[]{:S(2)}, u32[]{:S(2)}) collective-permute-start(bf16[1024,128]{1,0:T(8,128)(2,1)} %get-tuple-element.225), channel_id=1, source_target_pairs={{0,32},{32,64},{64,96},{96,128},{128,160},{160,192},{192,224},{224... | collective-permute-start | bytes 786440 | tf_op jit(solution)/shard_map/ppermute | solution.py:16
  58.8 63.9 %collective-permute-done = bf16[1024,128]{1,0:T(8,128)(2,1)S(1)} collective-permute-done((bf16[1024,128]{1,0:T(8,128)(2,1)S(1)}, bf16[1024,128]{1,0:T(8,128)(2,1)S(1)}, u32[]{:S(2)}, u32[]{:S(2)}) %collective-permute-start) | collective-permute-done | bytes 262176 | tf_op jit(solution)/shard_map/ppermute | solution.py:16
  122.7 1.1 fusion.100
  123.8 1.7 copy-done.6
  126.2 1.1 slice_bitcast_fusion.1
  127.3 42.7 %while.31 = (s32[]{:T(128)}, f32[1,1536,128]{2,1,0:T(8,128)}, f32[1,1536,128]{2,1,0:T(8,128)}, bf16[3,1,512,128]{3,2,1,0:T(8,128)(2,1)}, bf16[3,1,512,128]{3,2,1...) while((s32[]{:T(128)}, f32[1,1536,128]{2,1,0:T(8,128)}, ...), condition=%wide.region_16.17_spmd.clone, body=%wide.region_12.16_spmd.clone.sunk | while | flops 1218836992 | bytes 47988552 | solution.py:79
  127.3 1.7 fusion.149
  129.6 0.7 fusion.151
  130.9 0.6 copy-done.1
  131.7 1.7 fusion.154
  133.4 3.0 %fusion.155 = f32[1,1536,128]{2,1,0:T(8,128)} fusion(bf16[512,1536]{1,0:T(8,128)(2,1)} %fusion.154, f32[1,1536,128]{2,1,0:T(8,128)} %get-tuple-element.360, pred[]{:T(512)S(6)} %compare.11, bf16[3,1,512,128]{3,2,1,0:T(8,128)(2,1)} %get-tuple-element.376, s32[]{:T(128)S(6)} %copy.78), kind=kOutput, calls=%fused_computation.26.clone.1 | convolution fusion | flops 201916416 | bytes 3276805 | tf_op jit(solution)/shard_map/vmap()/while/body/eval_jaxpr/qk,qd->kd/dot_general | solution.py:45
  136.4 2.0 fusion.156
  138.4 0.7 bitcast_dynamic-update-slice_fusion.2
  139.1 2.2 fusion.157
  141.4 1.7 fusion.149
  143.7 0.7 fusion.151
  145.0 0.6 copy-done.1
  145.8 1.7 fusion.154
  147.5 3.2 %fusion.155 = f32[1,1536,128]{2,1,0:T(8,128)} fusion(bf16[512,1536]{1,0:T(8,128)(2,1)} %fusion.154, f32[1,1536,128]{2,1,0:T(8,128)} %get-tuple-element.360, pred[]{:T(512)S(6)} %compare.11, bf16[3,1,512,128]{3,2,1,0:T(8,128)(2,1)} %get-tuple-element.376, s32[]{:T(128)S(6)} %copy.78), kind=kOutput, calls=%fused_computation.26.clone.1 | convolution fusion | flops 201916416 | bytes 3276805 | tf_op jit(solution)/shard_map/vmap()/while/body/eval_jaxpr/qk,qd->kd/dot_general | solution.py:45
  150.7 2.0 fusion.156
  152.7 0.7 bitcast_dynamic-update-slice_fusion.2
  153.4 2.2 fusion.157
  155.7 1.7 fusion.149
  158.0 0.7 fusion.151
  159.3 0.6 copy-done.1
  160.1 1.7 fusion.154
  161.8 3.2 %fusion.155 = f32[1,1536,128]{2,1,0:T(8,128)} fusion(bf16[512,1536]{1,0:T(8,128)(2,1)} %fusion.154, f32[1,1536,128]{2,1,0:T(8,128)} %get-tuple-element.360, pred[]{:T(512)S(6)} %compare.11, bf16[3,1,512,128]{3,2,1,0:T(8,128)(2,1)} %get-tuple-element.376, s32[]{:T(128)S(6)} %copy.78), kind=kOutput, calls=%fused_computation.26.clone.1 | convolution fusion | flops 201916416 | bytes 3276805 | tf_op jit(solution)/shard_map/vmap()/while/body/eval_jaxpr/qk,qd->kd/dot_general | solution.py:45
  165.0 2.0 fusion.156
  167.0 0.7 bitcast_dynamic-update-slice_fusion.2
  167.7 2.2 fusion.157
  170.0 1.2 convert_element_type.152
  171.2 1.2 convert_element_type.151
  172.3 1.3 pad_maximum_fusion
  173.7 2.4 copy.54
  176.0 11.9 %all-to-all-start.2 = ((bf16[16,1,96,4,128]{4,3,2,1,0:T(4,128)(2,1)}), bf16[16,1,96,4,128]{4,3,2,1,0:T(4,128)(2,1)}, u32[]{:S(2)}, u32[]{:S(2)}) async-start(bf16[16,1,96,4,128]{4,3,2,1,0:T(4,128)(2,1)} %copy.54), calls=%async_computation.2 | async-start | bytes 3145728 | tf_op jit(solution)/shard_map/all_to_all | solution.py:101
  188.5 1.6 convolution_convert_fusion.1
  190.2 1.1 fusion.101
  192.4 1.6 convolution_convert_fusion.2
  195.2 1.3 collective-permute-start.3
  196.7 1.8 fusion.54
  199.0 1.8 fusion.55
  201.5 1.3 collective-permute-start.2
  203.4 0.6 fusion.60
  204.0 0.7 pad_maximum_fusion.5
  204.8 64.5 %collective-permute-done.3 = f32[1024,128]{1,0:T(8,128)S(1)} collective-permute-done((f32[1024,128]{1,0:T(8,128)S(1)}, f32[1024,128]{1,0:T(8,128)S(1)}, u32[]{:S(2)}, u32[]{:S(2)}) %collective-permute-start.3) | collective-permute-done | bytes 524320 | tf_op jit(solution)/shard_map/ppermute | solution.py:16
  269.3 10.1 %collective-permute-done.2 = f32[1024,128]{1,0:T(8,128)S(1)} collective-permute-done((f32[1024,128]{1,0:T(8,128)S(1)}, f32[1024,128]{1,0:T(8,128)S(1)}, u32[]{:S(2)}, u32[]{:S(2)}) %collective-permute-start.2) | collective-permute-done | bytes 524320 | tf_op jit(solution)/shard_map/ppermute | solution.py:16
  279.5 1.0 pad_maximum_fusion.2
  280.5 5.0 %gather_fusion.1 = bf16[1024,4,128]{2,1,0:T(4,128)(2,1)S(1)} fusion(bf16[1536,4,128]{2,1,0:T(4,128)(2,1)} %bitcast.29, s32[1024]{0:T(1024)S(1)} %broadcast_clamp_fusion), kind=kCustom, calls=%fused_computation.1 | custom fusion | bytes 2101248 | tf_op jit(solution)/shard_map/gather | solution.py:205
  286.4 0.7 copy.60
  287.1 1.0 copy.55
  (127 shorter events, 15.3 us)
Async XLA Ops:
  0.6 22.4 %copy-start.9 = (bf16[3,1024,128]{2,1,0:T(8,128)(2,1)S(1)}, bf16[3,1024,128]{2,1,0:T(8,128)(2,1)}, u32[]{:S(2)}) copy-start(bf16[3,1024,128]{2,1,0:T(8,128)(2,1)} %param.11) | copy-start | bytes 2359300
  5.7 30.4 %all-to-all-start = ((bf16[16,1,96]{2,1,0:T(2,128)(2,1)}), bf16[16,1,96]{2,1,0:T(2,128)(2,1)S(1)}, u32[]{:S(2)}, u32[]{:S(2)}) async-start(bf16[16,1,96]{2,1,0:T(2,128)(2,1)} %reshape.283), calls=%async_computation | async-start | bytes 16384 | tf_op jit(solution)/shard_map/all_to_all | solution.py:196
  32.0 16.2 %copy-start.10 = (bf16[3,1024,128]{2,1,0:T(8,128)(2,1)S(1)}, bf16[3,1024,128]{2,1,0:T(8,128)(2,1)}, u32[]{:S(2)}) copy-start(bf16[3,1024,128]{2,1,0:T(8,128)(2,1)} %param.9) | copy-start | bytes 2359300
  32.0 25.4 %copy-start.14 = (s32[1,1024]{1,0:T(1,128)S(1)}, s32[1,1024]{1,0:T(1,128)}, u32[]{:S(2)}) copy-start(s32[1,1024]{1,0:T(1,128)} %param.13) | copy-start | bytes 12292
  36.1 89.8 %all-to-all-start.1 = ((bf16[16,1,96,4,128]{4,3,2,1,0:T(4,128)(2,1)}), bf16[16,1,96,4,128]{4,3,2,1,0:T(4,128)(2,1)S(1)}, u32[]{:S(2)}, u32[]{:S(2)}) async-start(bf16[16,1,96,4,128]{4,3,2,1,0:T(4,128)(2,1)} %broadcast_select_fusion.1), calls=%async_computation.1 | async-start | bytes 3145728 | tf_op jit(solution)/shard_map/all_to_all | solution.py:189
  48.9 74.8 %copy-start.12 = (bf16[1024,128]{1,0:T(8,128)(2,1)}, bf16[1024,128]{1,0:T(8,128)(2,1)S(1)}, u32[]{:S(2)}) copy-start(bf16[1024,128]{1,0:T(8,128)(2,1)S(1)} %get-tuple-element.226) | copy-start | bytes 786436
  48.9 73.8 %collective-permute-start = (bf16[1024,128]{1,0:T(8,128)(2,1)S(1)}, bf16[1024,128]{1,0:T(8,128)(2,1)S(1)}, u32[]{:S(2)}, u32[]{:S(2)}) collective-permute-start(bf16[1024,128]{1,0:T(8,128)(2,1)S(1)} %get-tuple-element.226), channel_id=1, source_target_pairs={{0,32},{32,64},{64,96},{96,128},{128,160},{160,192},{192,224},{224... | collective-permute-start | bytes 786440 | tf_op jit(solution)/shard_map/ppermute | solution.py:16
  52.8 135.8 %collective-permute-start.1 = (bf16[1024,128]{1,0:T(8,128)(2,1)}, bf16[1024,128]{1,0:T(8,128)(2,1)}, u32[]{:S(2)}, u32[]{:S(2)}) collective-permute-start(bf16[1024,128]{1,0:T(8,128)(2,1)} %get-tuple-element.225), channel_id=1, source_target_pairs={{0,32},{32,64},{64,96},{96,128},{128,160},{160,192},{192,224},{224... | collective-permute-start | bytes 786440 | tf_op jit(solution)/shard_map/ppermute | solution.py:16
  122.7 1.1 copy-start.18
  123.8 1.7 copy-start.6
  130.3 1.2 copy-start.5
  130.9 0.7 copy-start.1
  133.4 3.0 %copy-start.3 = (f32[1,1536,128]{2,1,0:T(8,128)S(1)}, f32[1,1536,128]{2,1,0:T(8,128)}, u32[]{:S(2)}) copy-start(f32[1,1536,128]{2,1,0:T(8,128)} %get-tuple-element.361) | copy-start | bytes 2359300 | tf_op jit(solution)/shard_map/vmap()/while
  136.4 2.0 copy-start.2
  136.4 2.8 copy-start
  138.4 3.0 %copy-start.4 = (f32[1,1536,128]{2,1,0:T(8,128)}, f32[1,1536,128]{2,1,0:T(8,128)S(1)}, u32[]{:S(2)}) copy-start(f32[1,1536,128]{2,1,0:T(8,128)S(1)} %fusion.156) | copy-start | bytes 2359300 | tf_op jit(solution)/shard_map/vmap()/while
  144.4 1.2 copy-start.5
  145.0 0.7 copy-start.1
  147.5 3.2 %copy-start.3 = (f32[1,1536,128]{2,1,0:T(8,128)S(1)}, f32[1,1536,128]{2,1,0:T(8,128)}, u32[]{:S(2)}) copy-start(f32[1,1536,128]{2,1,0:T(8,128)} %get-tuple-element.361) | copy-start | bytes 2359300 | tf_op jit(solution)/shard_map/vmap()/while
  150.7 2.0 copy-start.2
  150.7 2.7 copy-start
  152.7 3.0 %copy-start.4 = (f32[1,1536,128]{2,1,0:T(8,128)}, f32[1,1536,128]{2,1,0:T(8,128)S(1)}, u32[]{:S(2)}) copy-start(f32[1,1536,128]{2,1,0:T(8,128)S(1)} %fusion.156) | copy-start | bytes 2359300 | tf_op jit(solution)/shard_map/vmap()/while
  158.7 1.2 copy-start.5
  159.2 0.7 copy-start.1
  161.8 3.2 %copy-start.3 = (f32[1,1536,128]{2,1,0:T(8,128)S(1)}, f32[1,1536,128]{2,1,0:T(8,128)}, u32[]{:S(2)}) copy-start(f32[1,1536,128]{2,1,0:T(8,128)} %get-tuple-element.361) | copy-start | bytes 2359300 | tf_op jit(solution)/shard_map/vmap()/while
  165.0 2.0 copy-start.2
  165.0 2.7 copy-start
  167.0 3.0 %copy-start.4 = (f32[1,1536,128]{2,1,0:T(8,128)}, f32[1,1536,128]{2,1,0:T(8,128)S(1)}, u32[]{:S(2)}) copy-start(f32[1,1536,128]{2,1,0:T(8,128)S(1)} %fusion.156) | copy-start | bytes 2359300 | tf_op jit(solution)/shard_map/vmap()/while
  173.6 14.3 %copy-start.7 = (f32[512,1536]{0,1:T(8,128)S(1)}, f32[512,1536]{0,1:T(8,128)}, u32[]{:S(2)}) copy-start(f32[512,1536]{0,1:T(8,128)} %copy-done.6) | copy-start | bytes 9437188
  176.0 104.4 %all-to-all-start.2 = ((bf16[16,1,96,4,128]{4,3,2,1,0:T(4,128)(2,1)}), bf16[16,1,96,4,128]{4,3,2,1,0:T(4,128)(2,1)}, u32[]{:S(2)}, u32[]{:S(2)}) async-start(bf16[16,1,96,4,128]{4,3,2,1,0:T(4,128)(2,1)} %copy.54), calls=%async_computation.2 | async-start | bytes 3145728 | tf_op jit(solution)/shard_map/all_to_all | solution.py:101
  187.9 2.2 copy-start.11
  187.9 2.2 copy-start.13
  188.0 2.2 copy-start.15
  188.0 2.2 copy-start.16
  188.0 2.2 copy-start.17
  188.0 2.2 copy-start.19
  191.8 2.1 copy-start.8
  195.2 74.1 %collective-permute-start.3 = (f32[1024,128]{1,0:T(8,128)S(1)}, f32[1024,128]{1,0:T(8,128)S(1)}, u32[]{:S(2)}, u32[]{:S(2)}) collective-permute-start(f32[1024,128]{1,0:T(8,128)S(1)} %pad_add_fusion), channel_id=1, source_target_pairs={{32,0},{64,32},{96,64},{128,96},{160,128},{192,160},{224,192},{256... | collective-permute-start | bytes 1572872 | tf_op jit(solution)/shard_map/ppermute | solution.py:16
  201.5 78.0 %collective-permute-start.2 = (f32[1024,128]{1,0:T(8,128)S(1)}, f32[1024,128]{1,0:T(8,128)S(1)}, u32[]{:S(2)}, u32[]{:S(2)}) collective-permute-start(f32[1024,128]{1,0:T(8,128)S(1)} %pad_add_fusion.1), channel_id=1, source_target_pairs={{32,0},{64,32},{96,64},{128,96},{160,128},{192,160},{224,192},{256... | collective-permute-start | bytes 1572872 | tf_op jit(solution)/shard_map/ppermute | solution.py:16
where the time goes:
time: 289 us; the launch traced here: 288 us
  waiting for transfers between devices  139 us (48%)
  starting transfers between devices  49.6 us (17%)
  matrix products  47.2 us (16%)
  local copies, waits for them, and re-layouts  27.2 us (9%)
  other arithmetic  24.2 us (8%)
    ppermute x4, waiting for transfers between devices, shifted(): return lax.ppermute(block, axis, route)  138 us
    all_to_all x1, starting transfers between devices, on_device(): lax.all_to_all(present.reshape(seq_count, per_owner, slot_cap), 'seq', sp...  15.2 us
    all_to_all x1, starting transfers between devices, on_device(): lax.all_to_all(buffer.reshape(seq_count, per_owner, slot_cap, 4, head_siz...  12 us
    all_to_all x1, starting transfers between devices, owner_work(): lax.all_to_all(arranged, 'seq', split_axis=0, concat_axis=0, tiled=True)  11.9 us
    dot_general x5, matrix products, key_terms(): jnp.einsum('qk,qd->kd', dscore, query_rows, preferred_element_type=jnp.fl...  10.5 us
    ppermute x4, starting transfers between devices, shifted(): return lax.ppermute(block, axis, route)  10.5 us
    dot_general x5, matrix products, attend_rows(): jnp.einsum('qd,kd->qk', grad_rows, value_rows, preferred_element_type=jnp...  8.72 us
    dot_general x5, matrix products, attend_rows(): jnp.dot(dscore, key_rows, preferred_element_type=jnp.float32) * factor  7.92 us
  transfers between devices with their start and end apart: 7, of which 3 were waited for; matrix products, arithmetic and copies ran while one was open for 29% of the time, Pallas kernels for 0%

commit v1 on v0

v1 whole, which is shorter than its diff:
```python
import jax
import jax.numpy as jnp
from jax import lax
from jax.experimental import pallas as pl
from jax.experimental.pallas import tpu as pltpu
from jax.sharding import PartitionSpec as P

WIN = 1024
SLOTS = 96
EMPTY = 512.0
masked_fill = -1e30


def dot_nn(a, b):
    return lax.dot_general(a, b, (((1,), (0,)), ((), ())), preferred_element_type=jnp.float32)


def dot_nt(a, b):
    return lax.dot_general(a, b, (((1,), (1,)), ((), ())), preferred_element_type=jnp.float32)


def dot_tn(a, b):
    return lax.dot_general(a, b, (((0,), (0,)), ((), ())), preferred_element_type=jnp.float32)


def softmax_grad(query, key, value, grad, factor, mask):
    scores = dot_nt(query, key)
    if mask is not None:
        scores = mask(scores)
    peak = jnp.max(scores, axis=1, keepdims=True)
    probs = jnp.exp((scores - peak) * factor)
    probs = probs * (1.0 / jnp.sum(probs, axis=1, keepdims=True))
    weights = probs.astype(jnp.bfloat16)
    output = dot_nn(weights, value).astype(jnp.bfloat16)
    delta = jnp.sum(
        grad.astype(jnp.float32) * output.astype(jnp.float32), axis=1, keepdims=True
    )
    dscores = (probs * (dot_nt(grad, value) - delta)).astype(jnp.bfloat16)
    dquery = (dot_nn(dscores, key) * factor).astype(jnp.bfloat16)
    return output, dquery, dscores, weights


def route_kernel(labels_ref, qkv_ref, grad_ref, buffer_ref, target_ref):
    tokens = labels_ref.shape[1]
    clusters = buffer_ref.shape[0]
    labels = labels_ref[...]
    block = 256
    lower = lax.broadcasted_iota(jnp.int32, (block, block), 0)
    upper = lax.broadcasted_iota(jnp.int32, (block, block), 1)
    triangle = (lower <= upper).astype(jnp.bfloat16)
    cluster_rows = lax.broadcasted_iota(jnp.int32, (clusters, block), 0)
    running = jnp.zeros((clusters, 1), jnp.float32)
    targets = []
    for start in range(0, tokens, block):
        part = labels[:, start : start + block]
        onehot = (cluster_rows == part).astype(jnp.float32)
        within = dot_nn(onehot.astype(jnp.bfloat16), triangle) + running
        rank = jnp.sum(within * onehot, axis=0, keepdims=True).astype(jnp.int32) - 1
        targets.append(part * SLOTS + rank)
        running = running + jnp.sum(onehot, axis=1, keepdims=True)
    target = jnp.concatenate(targets, axis=1)
    target_ref[...] = jnp.transpose(
        jnp.broadcast_to(target.astype(jnp.float32), (128, tokens))
    ).astype(jnp.int32)
    payload = jnp.concatenate([qkv_ref[0], qkv_ref[1], qkv_ref[2], grad_ref[...]], axis=1)
    head_size = grad_ref.shape[1]
    slot_rows = lax.broadcasted_iota(jnp.int32, (SLOTS, tokens), 0)
    fill_rows = lax.broadcasted_iota(jnp.int32, (SLOTS, head_size), 0)
    for cluster in range(clusters):
        select = (slot_rows + cluster * SLOTS == target).astype(jnp.float32).astype(jnp.bfloat16)
        rows = dot_nn(select, payload)
        count = running[cluster : cluster + 1, :].astype(jnp.int32)
        first = jnp.where(fill_rows < count, rows[:, :head_size], EMPTY)
        buffer_ref[cluster, :, :head_size] = first.astype(jnp.bfloat16)
        buffer_ref[cluster, :, head_size:] = rows[:, head_size:].astype(jnp.bfloat16)


def route(labels, qkv, grad, clusters):
    tokens, head_size = grad.shape
    return pl.pallas_call(
        route_kernel,
        out_shape=(
            jax.ShapeDtypeStruct((clusters, SLOTS, 4 * head_size), jnp.bfloat16),
            jax.ShapeDtypeStruct((tokens, 128), jnp.int32),
        ),
        compiler_params=pltpu.CompilerParams(vmem_limit_bytes=48 << 20),
        name="route",
    )(labels, qkv, grad)


def cluster_kernel(received_ref, result_ref, counts_vmem, counts_smem, rows_ref, out_ref, sem):
    sources = received_ref.shape[0]
    head_size = received_ref.shape[2] // 4
    tokens = rows_ref.shape[1] - SLOTS
    factor = head_size ** (-0.5)
    filled = []
    for source in range(sources):
        mark = received_ref[source, :, :head_size].astype(jnp.float32)
        filled.append(jnp.sum((mark < EMPTY).astype(jnp.float32), axis=0, keepdims=True))
    counts_vmem[...] = jnp.concatenate(filled, axis=0).astype(jnp.int32)
    copy = pltpu.make_async_copy(counts_vmem, counts_smem, sem)
    copy.start()
    copy.wait()
    starts = []
    start = 0
    for source in range(sources):
        starts.append(start)
        for part in range(4):
            lanes = slice(part * head_size, (part + 1) * head_size)
            rows_ref[part, pl.ds(start, SLOTS), :] = received_ref[source, :, lanes].astype(
                jnp.float32
            )
        start = jnp.minimum(start + counts_smem[source, 0], tokens)
    block = 256
    key = rows_ref[1, :tokens, :].astype(jnp.bfloat16)
    value = rows_ref[2, :tokens, :].astype(jnp.bfloat16)
    key_grad = jnp.zeros((tokens, head_size), jnp.float32)
    value_grad = jnp.zeros((tokens, head_size), jnp.float32)
    for row in range(0, tokens, block):
        query = rows_ref[0, row : row + block, :].astype(jnp.bfloat16)
        grad = rows_ref[3, row : row + block, :].astype(jnp.bfloat16)
        output, dquery, dscores, weights = softmax_grad(query, key, value, grad, factor, None)
        out_ref[0, row : row + block, :] = output.astype(jnp.float32)
        out_ref[1, row : row + block, :] = dquery.astype(jnp.float32)
        key_grad = key_grad + dot_tn(dscores, query)
        value_grad = value_grad + dot_tn(weights, grad)
    out_ref[2, :tokens, :] = key_grad * factor
    out_ref[3, :tokens, :] = value_grad
    out_ref[:, tokens:, :] = jnp.zeros((4, SLOTS, head_size), jnp.float32)
    for source in range(sources):
        for part in range(4):
            lanes = slice(part * head_size, (part + 1) * head_size)
            result_ref[source, :, lanes] = out_ref[part, pl.ds(starts[source], SLOTS), :].astype(
                jnp.bfloat16
            )


def cluster_attention(received, tokens):
    sources, slots, width = received.shape
    return pl.pallas_call(
        cluster_kernel,
        out_shape=jax.ShapeDtypeStruct(received.shape, jnp.bfloat16),
        scratch_shapes=[
            pltpu.VMEM((sources, 128), jnp.int32),
            pltpu.SMEM((sources, 128), jnp.int32),
            pltpu.VMEM((4, tokens + SLOTS, width // 4), jnp.float32),
            pltpu.VMEM((4, tokens + SLOTS, width // 4), jnp.float32),
            pltpu.SemaphoreType.DMA,
        ],
        compiler_params=pltpu.CompilerParams(vmem_limit_bytes=56 << 20),
        name="cluster",
    )(received)


def unroute_kernel(returned_ref, target_ref, output_ref, grads_ref):
    clusters = returned_ref.shape[0]
    tokens, head_size = output_ref.shape
    slots = clusters * SLOTS
    rows = returned_ref[...].reshape(slots, 4 * head_size)
    block = 256
    lanes = lax.broadcasted_iota(jnp.int32, (block, 128), 1)
    for row in range(0, tokens, block):
        target = target_ref[row : row + block, :]
        select = jnp.concatenate(
            [
                (lanes + lane == target).astype(jnp.float32).astype(jnp.bfloat16)
                for lane in range(0, slots, 128)
            ],
            axis=1,
        )
        picked = dot_nn(select, rows).astype(jnp.bfloat16)
        output_ref[row : row + block, :] = picked[:, :head_size]
        for part in range(3):
            grads_ref[part, row : row + block, :] = picked[
                :, (part + 1) * head_size : (part + 2) * head_size
            ]


def unroute(returned, target, head_size):
    tokens = target.shape[0]
    return pl.pallas_call(
        unroute_kernel,
        out_shape=(
            jax.ShapeDtypeStruct((tokens, head_size), jnp.bfloat16),
            jax.ShapeDtypeStruct((3, tokens, head_size), jnp.bfloat16),
        ),
        compiler_params=pltpu.CompilerParams(vmem_limit_bytes=48 << 20),
        name="unroute",
    )(returned, target)


def local_kernel(
    index_ref, qkv_ref, grad_ref, prev_ref, output_ref, dquery_ref, own_ref, late_ref, keys, values, key_acc, value_acc
):
    tokens, head_size = grad_ref.shape
    factor = head_size ** (-0.5)
    block = 256
    span = WIN + block
    keys[:tokens, :] = prev_ref[0]
    keys[tokens:, :] = qkv_ref[1]
    values[:tokens, :] = prev_ref[1]
    values[tokens:, :] = qkv_ref[2]
    key_acc[...] = jnp.zeros_like(key_acc)
    value_acc[...] = jnp.zeros_like(value_acc)
    rows = lax.broadcasted_iota(jnp.int32, (block, block), 0)
    columns = lax.broadcasted_iota(jnp.int32, (block, block), 1)
    whole = lax.broadcasted_iota(jnp.int32, (block, span), 1)
    first_key = jnp.where(index_ref[0] == 0, tokens, 0)

    for row in range(0, tokens, block):

        def mask(scores, row=row):
            head = jnp.where(columns > rows, scores[:, :block], masked_fill)
            tail = jnp.where(columns <= rows, scores[:, span - block :], masked_fill)
            joined = jnp.concatenate([head, scores[:, block : span - block], tail], axis=1)
            return jnp.where(whole + row >= first_key, joined, masked_fill)

        query = qkv_ref[0, row : row + block, :]
        grad = grad_ref[row : row + block, :]
        key = keys[row : row + span, :]
        value = values[row : row + span, :]
        output, dquery, dscores, weights = softmax_grad(query, key, value, grad, factor, mask)
        output_ref[row : row + block, :] = output
        dquery_ref[row : row + block, :] = dquery
        key_acc[row : row + span, :] += dot_tn(dscores, query)
        value_acc[row : row + span, :] += dot_tn(weights, grad)
    late_ref[0] = (key_acc[:tokens, :] * factor).astype(jnp.bfloat16)
    late_ref[1] = value_acc[:tokens, :].astype(jnp.bfloat16)
    own_ref[0] = key_acc[tokens:, :] * factor
    own_ref[1] = value_acc[tokens:, :]


def local_attention(index, qkv, grad, prev):
    tokens, head_size = grad.shape
    vmem = pl.BlockSpec(memory_space=pltpu.VMEM)
    return pl.pallas_call(
        local_kernel,
        out_shape=(
            jax.ShapeDtypeStruct((tokens, head_size), jnp.bfloat16),
            jax.ShapeDtypeStruct((tokens, head_size), jnp.bfloat16),
            jax.ShapeDtypeStruct((2, tokens, head_size), jnp.float32),
            jax.ShapeDtypeStruct((2, tokens, head_size), jnp.bfloat16),
        ),
        in_specs=[pl.BlockSpec(memory_space=pltpu.SMEM), vmem, vmem, vmem],
        scratch_shapes=[
            pltpu.VMEM((2 * tokens, head_size), jnp.bfloat16),
            pltpu.VMEM((2 * tokens, head_size), jnp.bfloat16),
            pltpu.VMEM((2 * tokens, head_size), jnp.float32),
            pltpu.VMEM((2 * tokens, head_size), jnp.float32),
        ],
        compiler_params=pltpu.CompilerParams(vmem_limit_bytes=56 << 20),
        name="local",
    )(index, qkv, grad, prev)


def shifted(block, distance):
    devices = range(lax.axis_size("seq"))
    return lax.ppermute(
        block, "seq", [(i - distance, i) for i in devices if i - distance in devices]
    )


def on_device(local_qkv, local_grad, routed_qkv, routed_grad, cluster_ids):
    tokens, head_size = local_grad.shape
    clusters = lax.axis_size("seq")
    prev = shifted(local_qkv[1:], 1)
    buffer, target = route(cluster_ids, routed_qkv, routed_grad, clusters)
    received = lax.all_to_all(buffer, "seq", split_axis=0, concat_axis=0, tiled=True)
    index = lax.axis_index("seq").astype(jnp.int32).reshape(1)
    local_out, dquery, own, late = local_attention(index, local_qkv, local_grad, prev)
    late = shifted(late, -1)
    returned = lax.all_to_all(
        cluster_attention(received, tokens), "seq", split_axis=0, concat_axis=0, tiled=True
    )
    joined = (own + late.astype(jnp.float32)).astype(jnp.bfloat16)
    local_dqkv = jnp.concatenate([dquery[None], joined], axis=0)
    routed_out, routed_dqkv = unroute(returned, target, head_size)
    return (local_out, local_dqkv, routed_out, routed_dqkv)


def solution(mesh):
    rows = P(("dp", "seq"), "head")
    stacked = P(None, ("dp", "seq"), "head")
    return jax.shard_map(
        on_device,
        mesh=mesh,
        in_specs=(stacked, rows, stacked, rows, P("head", ("dp", "seq"))),
        out_specs=(rows, stacked, rows, stacked),
        check_vma=False,
    )
```

time: 289 us -> 221 us (0.76)
  blocking collectives: 0 us -> 89.1 us
  waiting for transfers between devices: 139 us -> 89.2 us
  matrix products: 47.2 us -> 0 us
  starting transfers between devices: 49.6 us -> 11.9 us
  local copies, waits for them, and re-layouts: 27.2 us -> 3.6 us
  Pallas kernels: 0 us -> 23.1 us
  other arithmetic: 24.2 us -> 2.28 us
    all_to_all x0 -> x1, blocking collectives: none -> 89.1 us  [on_device(): lax.all_to_all(buffer, 'seq', split_axis=0, concat_axis=0, tiled=True)]
    ppermute x4 -> x2, waiting for transfers between devices: 138 us -> 89.2 us  [shifted(): lax.ppermute(block, 'seq', [(i - distance, i) for i in devices if i - dis...]
    dot_general x32 -> x0, matrix products: 47.2 us -> none  [the longest x5 10.5 us: key_terms(): jnp.einsum('qk,qd->kd', dscore, query_rows, preferred_element_type=jnp.fl...]
    all_to_all x3 -> x1, starting transfers between devices: 39.1 us -> 6.44 us  [on_device(): lax.all_to_all(cluster_attention(received, tokens), 'seq', split_axis=0,...]
    pallas_call x0 -> x4, Pallas kernels: none -> 23.1 us  [the longest x1 8.8 us: cluster_attention(): pl.pallas_call(cluster_kernel, out_shape=jax.ShapeDtypeStruct(received.sh...]
    gather x2 -> x0, local copies, waits for them, and re-layouts: 10.1 us -> none  [the longest x1 5.12 us: on_device(): payload[source]]
    ppermute x4 -> x2, starting transfers between devices: 10.5 us -> 5.45 us  [shifted(): lax.ppermute(block, 'seq', [(i - distance, i) for i in devices if i - dis...]
    another operation x6 -> x0, local copies, waits for them, and re-layouts: 5.02 us -> none  [the longest x5 2.63 us: on_device(): jnp.stack([routed_qkv[0], routed_qkv[1], routed_qkv[2], routed_grad], axi...]
  transfers between devices with their start and end apart: 7 -> 3, of which waited for: 3 -> 2; matrix products, arithmetic and copies ran while one was open for 29% -> 1% of each run, Pallas kernels for 0% -> 4%
where the time goes in v1:
time: 221 us; the launch traced here: 220 us
  waiting for transfers between devices  89.2 us (40%)
  blocking collectives  89.1 us (40%)
  Pallas kernels  23.1 us (10%)
  starting transfers between devices  11.9 us (5%)
  local copies, waits for them, and re-layouts  3.6 us (2%)
  other arithmetic  2.28 us (1%)
    ppermute x2, waiting for transfers between devices, shifted(): lax.ppermute(block, 'seq', [(i - distance, i) for i in devices if i - dis...  89.2 us
    all_to_all x1, blocking collectives, on_device(): lax.all_to_all(buffer, 'seq', split_axis=0, concat_axis=0, tiled=True)  89.1 us
    pallas_call x1, Pallas kernels, cluster_attention(): pl.pallas_call(cluster_kernel, out_shape=jax.ShapeDtypeStruct(received.sh...  8.8 us
    pallas_call x1, Pallas kernels, local_attention(): pl.pallas_call(local_kernel, out_shape=(jax.ShapeDtypeStruct((tokens, hea...  8.59 us
    all_to_all x1, starting transfers between devices, on_device(): lax.all_to_all(cluster_attention(received, tokens), 'seq', split_axis=0,...  6.44 us
    ppermute x2, starting transfers between devices, shifted(): lax.ppermute(block, 'seq', [(i - distance, i) for i in devices if i - dis...  5.45 us
  transfers between devices with their start and end apart: 3, of which 2 were waited for; matrix products, arithmetic and copies ran while one was open for 1% of the time, Pallas kernels for 4%

profile of v1, /device:TPU:24, one launch (start us, length us, event | category | flops | bytes accessed | tf_op | source)
XLA Modules:
  0.0 219.9 jit_solution(17023230876304552033)
XLA Ops:
  0.6 0.0 copy-start
  0.6 1.1 copy-done
  1.8 0.0 copy-start.1
  1.8 0.9 copy-done.1
  2.7 0.0 copy-start.2
  2.7 0.7 copy-done.2
  3.4 3.0 %route.1 = (bf16[16,96,512]{2,1,0:T(8,128)(2,1)S(1)}, s32[1024,128]{1,0:T(8,128)S(1)}) custom-call(s32[1,1024]{1,0:T(1,128)S(1)} %copy-done.2, bf16[3,1024,128]{2,1,0:T(8,128)(2,1)S(1)} %copy-done, bf16[1024,128]{1,0:T(8,128)(2,1)S(1)} %copy-done.1), custom_call_target="tpu_custom_call" | custom-call | tf_op jit(solution)/shard_map/route/pallas_call | solution.py:80
  6.4 89.1 %all_to_all.10.received_ref = bf16[16,96,512]{2,1,0:T(8,128)(2,1)} all-to-all(bf16[16,96,512]{2,1,0:T(8,128)(2,1)S(1)} %get-tuple-element.16), channel_id=1, replica_groups=mesh['seq'=16,'head'=16,'dp'=2] {'seq'}, dimensions={0} | all-to-all | bytes 3145728 | tf_op jit(solution)/shard_map/all_to_all | solution.py:268
  95.5 8.8 %cluster.1 = bf16[16,96,512]{2,1,0:T(8,128)(2,1)} custom-call(bf16[16,96,512]{2,1,0:T(8,128)(2,1)} %all_to_all.10.received_ref), custom_call_target="tpu_custom_call" | custom-call | tf_op jit(solution)/shard_map/cluster/pallas_call | solution.py:140
  104.3 0.0 copy-start.3
  104.3 6.4 %all-to-all-start.1 = ((bf16[16,96,512]{2,1,0:T(8,128)(2,1)}), bf16[16,96,512]{2,1,0:T(8,128)(2,1)S(1)}, u32[]{:S(2)}, u32[]{:S(2)}) async-start(bf16[16,96,512]{2,1,0:T(8,128)(2,1)} %cluster.1), calls=%async_computation.1 | async-start | bytes 3145728 | tf_op jit(solution)/shard_map/all_to_all | solution.py:272
  110.8 0.0 copy-done.3
  110.8 4.0 %collective-permute-start = (bf16[2,1024,128]{2,1,0:T(8,128)(2,1)S(1)}, bf16[2,1024,128]{2,1,0:T(8,128)(2,1)S(1)}, u32[]{:S(2)}, u32[]{:S(2)}) collective-permute-start(bf16[2,1024,128]{2,1,0:T(8,128)(2,1)S(1)} %slice.3), channel_id=1, source_target_pairs={{0,32},{32,64},{64,96},{96,128},{128,160},{160,192},{192,224},{224... | collective-permute-start | bytes 1572872 | tf_op jit(solution)/shard_map/ppermute | solution.py:258
  114.9 74.8 %collective-permute-done.prev_ref = bf16[2,1024,128]{2,1,0:T(8,128)(2,1)S(1)} collective-permute-done((bf16[2,1024,128]{2,1,0:T(8,128)(2,1)S(1)}, bf16[2,1024,128]{2,1,0:T(8,128)(2,1)S(1)}, u32[]{:S(2)}, u32[]{:S(2)}) %collective-permute-start) | collective-permute-done | bytes 524320 | tf_op jit(solution)/shard_map/ppermute | solution.py:258
  189.7 0.0 copy-start.4
  189.7 0.8 copy-done.4
  190.5 8.6 %local.1 = (bf16[1024,128]{1,0:T(8,128)(2,1)}, bf16[1024,128]{1,0:T(8,128)(2,1)}, f32[2,1024,128]{2,1,0:T(8,128)}, bf16[2,1024,128]{2,1,0:T(8,128)(2,1)}) custom-call(s32[1]{0:T(128)} %bitcast.index_ref, bf16[3,1024,128]{2,1,0:T(8,128)(2,1)} %qkv_ref.2, bf16[1024,128]{1,0:T(8,128)(2,1)} %grad_ref.2, bf16[2,1024,128]{2,1,0:T(8,128)(2,1)} %copy-done.4), custom_call_target="tpu_custom_call" | custom-call | tf_op jit(solution)/shard_map/local/pallas_call | solution.py:236
  199.1 0.0 copy-start.5
  199.1 1.4 collective-permute-start.1
  200.5 14.4 %collective-permute-done.1 = bf16[2,1024,128]{2,1,0:T(8,128)(2,1)S(1)} collective-permute-done((bf16[2,1024,128]{2,1,0:T(8,128)(2,1)}, bf16[2,1024,128]{2,1,0:T(8,128)(2,1)S(1)}, u32[]{:S(2)}, u32[]{:S(2)}) %collective-permute-start.1) | collective-permute-done | bytes 524320 | tf_op jit(solution)/shard_map/ppermute | solution.py:258
  214.9 1.3 add_convert_fusion
  216.2 0.0 copy-done.5
  216.2 0.9 pad_maximum_fusion
  217.2 0.0 all-to-all-done.1.returned_ref
  217.2 2.8 %unroute.1 = (bf16[1024,128]{1,0:T(8,128)(2,1)}, bf16[3,1024,128]{2,1,0:T(8,128)(2,1)}) custom-call(bf16[16,96,512]{2,1,0:T(8,128)(2,1)S(1)} %all-to-all-done.1.returned_ref, s32[1024,128]{1,0:T(8,128)S(1)} %get-tuple-element.17.target_ref), custom_call_target="tpu_custom_call" | custom-call | tf_op jit(solution)/shard_map/unroute/pallas_call | solution.py:181
  (1 shorter events, 0.0 us)
Async XLA Ops:
  0.6 1.1 copy-start
  1.8 0.9 copy-start.1
  2.7 0.7 copy-start.2
  104.3 6.5 %copy-start.3 = (bf16[3,1024,128]{2,1,0:T(8,128)(2,1)S(1)}, bf16[3,1024,128]{2,1,0:T(8,128)(2,1)}, u32[]{:S(2)}) copy-start(bf16[3,1024,128]{2,1,0:T(8,128)(2,1)} %qkv_ref.2) | copy-start | bytes 2359300
  104.3 112.9 %all-to-all-start.1 = ((bf16[16,96,512]{2,1,0:T(8,128)(2,1)}), bf16[16,96,512]{2,1,0:T(8,128)(2,1)S(1)}, u32[]{:S(2)}, u32[]{:S(2)}) async-start(bf16[16,96,512]{2,1,0:T(8,128)(2,1)} %cluster.1), calls=%async_computation.1 | async-start | bytes 3145728 | tf_op jit(solution)/shard_map/all_to_all | solution.py:272
  110.8 78.9 %collective-permute-start = (bf16[2,1024,128]{2,1,0:T(8,128)(2,1)S(1)}, bf16[2,1024,128]{2,1,0:T(8,128)(2,1)S(1)}, u32[]{:S(2)}, u32[]{:S(2)}) collective-permute-start(bf16[2,1024,128]{2,1,0:T(8,128)(2,1)S(1)} %slice.3), channel_id=1, source_target_pairs={{0,32},{32,64},{64,96},{96,128},{128,160},{160,192},{192,224},{224... | collective-permute-start | bytes 1572872 | tf_op jit(solution)/shard_map/ppermute | solution.py:258
  189.7 0.8 copy-start.4
  199.1 17.1 %copy-start.5 = (bf16[1024,128]{1,0:T(8,128)(2,1)S(1)}, bf16[1024,128]{1,0:T(8,128)(2,1)}, u32[]{:S(2)}) copy-start(bf16[1024,128]{1,0:T(8,128)(2,1)} %get-tuple-element.13) | copy-start | bytes 786436
  199.1 15.8 %collective-permute-start.1 = (bf16[2,1024,128]{2,1,0:T(8,128)(2,1)}, bf16[2,1024,128]{2,1,0:T(8,128)(2,1)S(1)}, u32[]{:S(2)}, u32[]{:S(2)}) collective-permute-start(bf16[2,1024,128]{2,1,0:T(8,128)(2,1)} %get-tuple-element.15), channel_id=1, source_target_pairs={{32,0},{64,32},{96,64},{128,96},{160,128},{192,160},{224,192},{256... | collective-permute-start | bytes 1572872 | tf_op jit(solution)/shard_map/ppermute | solution.py:258

commit v2 on v1

--- a/solution.py
+++ b/solution.py
@@ -83,7 +83,7 @@
             jax.ShapeDtypeStruct((clusters, SLOTS, 4 * head_size), jnp.bfloat16),
             jax.ShapeDtypeStruct((tokens, 128), jnp.int32),
         ),
-        compiler_params=pltpu.CompilerParams(vmem_limit_bytes=48 << 20),
+        compiler_params=pltpu.CompilerParams(vmem_limit_bytes=20 << 20),
         name="route",
     )(labels, qkv, grad)
 
@@ -137,9 +137,12 @@
 
 def cluster_attention(received, tokens):
     sources, slots, width = received.shape
+    vmem = pl.BlockSpec(memory_space=pltpu.VMEM)
     return pl.pallas_call(
         cluster_kernel,
         out_shape=jax.ShapeDtypeStruct(received.shape, jnp.bfloat16),
+        in_specs=[vmem],
+        out_specs=vmem,
         scratch_shapes=[
             pltpu.VMEM((sources, 128), jnp.int32),
             pltpu.SMEM((sources, 128), jnp.int32),
@@ -147,7 +150,7 @@
             pltpu.VMEM((4, tokens + SLOTS, width // 4), jnp.float32),
             pltpu.SemaphoreType.DMA,
         ],
-        compiler_params=pltpu.CompilerParams(vmem_limit_bytes=56 << 20),
+        compiler_params=pltpu.CompilerParams(vmem_limit_bytes=28 << 20),
         name="cluster",
     )(received)
 
@@ -184,7 +187,8 @@
             jax.ShapeDtypeStruct((tokens, head_size), jnp.bfloat16),
             jax.ShapeDtypeStruct((3, tokens, head_size), jnp.bfloat16),
         ),
-        compiler_params=pltpu.CompilerParams(vmem_limit_bytes=48 << 20),
+        in_specs=[pl.BlockSpec(memory_space=pltpu.VMEM)] * 2,
+        compiler_params=pltpu.CompilerParams(vmem_limit_bytes=20 << 20),
         name="unroute",
     )(returned, target)
 
@@ -248,7 +252,7 @@
             pltpu.VMEM((2 * tokens, head_size), jnp.float32),
             pltpu.VMEM((2 * tokens, head_size), jnp.float32),
         ],
-        compiler_params=pltpu.CompilerParams(vmem_limit_bytes=56 << 20),
+        compiler_params=pltpu.CompilerParams(vmem_limit_bytes=28 << 20),
         name="local",
     )(index, qkv, grad, prev)
 
@@ -260,22 +264,48 @@
     )
 
 
-def on_device(local_qkv, local_grad, routed_qkv, routed_grad, cluster_ids):
+def exchange(block):
+    return lax.all_to_all(block, "seq", split_axis=0, concat_axis=0, tiled=True)
+
+
+def routed_first(local_qkv, local_grad, routed_qkv, routed_grad, cluster_ids):
     tokens, head_size = local_grad.shape
-    clusters = lax.axis_size("seq")
-    prev = shifted(local_qkv[1:], 1)
-    buffer, target = route(cluster_ids, routed_qkv, routed_grad, clusters)
-    received = lax.all_to_all(buffer, "seq", split_axis=0, concat_axis=0, tiled=True)
+    buffer, target = route(cluster_ids, routed_qkv, routed_grad, lax.axis_size("seq"))
+    received = exchange(buffer)
+    halo, buffer = lax.optimization_barrier((local_qkv[1:], buffer))
+    prev = shifted(halo, 1)
+    result = cluster_attention(received, tokens)
+    result, prev = lax.optimization_barrier((result, prev))
+    returned = exchange(result)
     index = lax.axis_index("seq").astype(jnp.int32).reshape(1)
     local_out, dquery, own, late = local_attention(index, local_qkv, local_grad, prev)
     late = shifted(late, -1)
-    returned = lax.all_to_all(
-        cluster_attention(received, tokens), "seq", split_axis=0, concat_axis=0, tiled=True
-    )
     joined = (own + late.astype(jnp.float32)).astype(jnp.bfloat16)
     local_dqkv = jnp.concatenate([dquery[None], joined], axis=0)
     routed_out, routed_dqkv = unroute(returned, target, head_size)
     return (local_out, local_dqkv, routed_out, routed_dqkv)
+
+
+def local_first(local_qkv, local_grad, routed_qkv, routed_grad, cluster_ids):
+    tokens, head_size = local_grad.shape
+    prev = shifted(local_qkv[1:], 1)
+    buffer, target = route(cluster_ids, routed_qkv, routed_grad, lax.axis_size("seq"))
+    index = lax.axis_index("seq").astype(jnp.int32).reshape(1)
+    local_out, dquery, own, late = local_attention(index, local_qkv, local_grad, prev)
+    buffer, late = lax.optimization_barrier((buffer, late))
+    received = exchange(buffer)
+    late = shifted(late, -1)
+    result = cluster_attention(received, tokens)
+    result, late = lax.optimization_barrier((result, late))
+    returned = exchange(result)
+    joined = (own + late.astype(jnp.float32)).astype(jnp.bfloat16)
+    local_dqkv = jnp.concatenate([dquery[None], joined], axis=0)
+    routed_out, routed_dqkv = unroute(returned, target, head_size)
+    return (local_out, local_dqkv, routed_out, routed_dqkv)
+
+
+def on_device(*arrays):
+    return lax.cond(lax.axis_index("dp") == 0, routed_first, local_first, *arrays)
 
 
 def solution(mesh):

time: 221 us -> 190 us (0.86)
  blocking collectives: 89.1 us -> 0 us
  waiting for transfers between devices: 89.2 us -> 131 us
  starting transfers between devices: 11.9 us -> 33.3 us
  local copies, waits for them, and re-layouts: 3.6 us -> 0.83 us
    all_to_all x1 -> x0, blocking collectives: 89.1 us -> none  [on_device(): lax.all_to_all(buffer, 'seq', split_axis=0, concat_axis=0, tiled=True)]
    all_to_all x1 -> x2, waiting for transfers between devices: 0.01 us -> 56.2 us  [exchange(): return lax.all_to_all(block, 'seq', split_axis=0, concat_axis=0, tiled=True)]
    all_to_all x1 -> x2, starting transfers between devices: 6.44 us -> 28.2 us  [exchange(): return lax.all_to_all(block, 'seq', split_axis=0, concat_axis=0, tiled=True)]
    ppermute x2, waiting for transfers between devices: 89.2 us -> 74.6 us  [shifted(): lax.ppermute(block, 'seq', [(i - distance, i) for i in devices if i - dis...]
    unnamed x12 -> x0, local copies, waits for them, and re-layouts: 3.56 us -> none
    pallas_call x1, Pallas kernels: 2.96 us -> 5.38 us  [route(): pl.pallas_call(route_kernel, out_shape=(jax.ShapeDtypeStruct((clusters, S...]
  transfers between devices with their start and end apart: 3 -> 4, of which waited for: 2 -> 3; matrix products, arithmetic and copies ran while one was open for 1% -> 1% of each run, Pallas kernels for 4% -> 8%
where the time goes in v2:
time: 190 us
  waiting for transfers between devices  131 us (69%)
  starting transfers between devices  33.3 us (18%)
  Pallas kernels  22.7 us (12%)
    ppermute x2, waiting for transfers between devices, shifted(): lax.ppermute(block, 'seq', [(i - distance, i) for i in devices if i - dis...  74.6 us
    all_to_all x2, waiting for transfers between devices, exchange(): return lax.all_to_all(block, 'seq', split_axis=0, concat_axis=0, tiled=True)  56.2 us
    all_to_all x2, starting transfers between devices, exchange(): return lax.all_to_all(block, 'seq', split_axis=0, concat_axis=0, tiled=True)  28.2 us
    pallas_call x1, Pallas kernels, cluster_attention(): pl.pallas_call(cluster_kernel, out_shape=jax.ShapeDtypeStruct(received.sh...  7.37 us
    pallas_call x1, Pallas kernels, local_attention(): pl.pallas_call(local_kernel, out_shape=(jax.ShapeDtypeStruct((tokens, hea...  7.18 us
    pallas_call x1, Pallas kernels, route(): pl.pallas_call(route_kernel, out_shape=(jax.ShapeDtypeStruct((clusters, S...  5.38 us
    ppermute x2, starting transfers between devices, shifted(): lax.ppermute(block, 'seq', [(i - distance, i) for i in devices if i - dis...  5.13 us
  transfers between devices with their start and end apart: 4, of which 3 were waited for; matrix products, arithmetic and copies ran while one was open for 1% of the time, Pallas kernels for 8%

profile of v2, /device:TPU:24, one launch (start us, length us, event | category | flops | bytes accessed | tf_op | source)
XLA Modules:
  0.0 189.6 jit_solution(12325914141707123924)
XLA Ops:
  0.6 189.0 %conditional.1 = (bf16[1024,128]{1,0:T(8,128)(2,1)}, bf16[1024,128]{1,0:T(8,128)(2,1)}, bf16[3,1024,128]{2,1,0:T(8,128)(2,1)}, bf16[3,1024,128]{2,1,0:T(8,128)(2,1)}) conditional(s32[]{:T(128)} %convert_element_type.15, (bf16[3,1024,128]{2,1,0:T(8,128)(2,1)}, bf16[1024,128]{1,0:T(8,128)(2,1)}, s32[1,1024]{1,0:T(1,128)}, ...), branch_computations={%region_0.0_spmd, %region_1.0_spmd} | conditional | flops 1179651 | bytes 24641828 | solution.py:308
  0.9 5.4 %route.3 = (bf16[16,96,512]{2,1,0:T(8,128)(2,1)}, s32[1024,128]{1,0:T(8,128)S(1)}) custom-call(s32[1,1024]{1,0:T(1,128)} %get-tuple-element.39.labels_ref, bf16[3,1024,128]{2,1,0:T(8,128)(2,1)} %get-tuple-element.40.qkv_ref, bf16[1024,128]{1,0:T(8,128)(2,1)} %get-tuple-element.41.grad_ref), custom_call_target="tpu_custom_call" | custom-call | tf_op jit(solution)/shard_map/cond/branch_1_fun/route/pallas_call | solution.py:80
  6.2 0.0 copy-start.2
  6.3 15.3 %all-to-all-start.2 = ((bf16[16,96,512]{2,1,0:T(8,128)(2,1)}), bf16[16,96,512]{2,1,0:T(8,128)(2,1)S(1)}, u32[]{:S(2)}, u32[]{:S(2)}) async-start(bf16[16,96,512]{2,1,0:T(8,128)(2,1)} %get-tuple-element.42), calls=%async_computation.2 | async-start | bytes 3145728 | tf_op jit(solution)/shard_map/cond/branch_1_fun/all_to_all | solution.py:268
  21.6 0.0 copy-done.2
  21.6 0.8 slice.5
  22.4 3.8 %collective-permute-start.2 = (bf16[2,1024,128]{2,1,0:T(8,128)(2,1)}, bf16[2,1024,128]{2,1,0:T(8,128)(2,1)S(1)}, u32[]{:S(2)}, u32[]{:S(2)}) collective-permute-start(bf16[2,1024,128]{2,1,0:T(8,128)(2,1)} %slice.5), channel_id=1, source_target_pairs={{0,32},{32,64},{64,96},{96,128},{128,160},{160,192},{192,224},{224... | collective-permute-start | bytes 1572872 | tf_op jit(solution)/shard_map/cond/branch_1_fun/ppermute | solution.py:262
  26.3 56.2 %all-to-all-done.2.received_ref = bf16[16,96,512]{2,1,0:T(8,128)(2,1)S(1)} async-done(((bf16[16,96,512]{2,1,0:T(8,128)(2,1)}), bf16[16,96,512]{2,1,0:T(8,128)(2,1)S(1)}, u32[]{:S(2)}, u32[]{:S(2)}) %all-to-all-start.2) | async-done | bytes 1572896 | tf_op jit(solution)/shard_map/cond/branch_1_fun/all_to_all | solution.py:268
  82.5 7.4 %cluster.3 = bf16[16,96,512]{2,1,0:T(8,128)(2,1)} custom-call(bf16[16,96,512]{2,1,0:T(8,128)(2,1)S(1)} %all-to-all-done.2.received_ref), custom_call_target="tpu_custom_call" | custom-call | tf_op jit(solution)/shard_map/cond/branch_1_fun/cluster/pallas_call | solution.py:141
  89.9 6.2 %collective-permute-done.2.prev_ref = bf16[2,1024,128]{2,1,0:T(8,128)(2,1)S(1)} collective-permute-done((bf16[2,1024,128]{2,1,0:T(8,128)(2,1)}, bf16[2,1024,128]{2,1,0:T(8,128)(2,1)S(1)}, u32[]{:S(2)}, u32[]{:S(2)}) %collective-permute-start.2) | collective-permute-done | bytes 524320 | tf_op jit(solution)/shard_map/cond/branch_1_fun/ppermute | solution.py:262
  96.1 12.9 %all-to-all-start.3 = ((bf16[16,96,512]{2,1,0:T(8,128)(2,1)}), bf16[16,96,512]{2,1,0:T(8,128)(2,1)S(1)}, u32[]{:S(2)}, u32[]{:S(2)}) async-start(bf16[16,96,512]{2,1,0:T(8,128)(2,1)} %cluster.3), calls=%async_computation.3 | async-start | bytes 3145728 | tf_op jit(solution)/shard_map/cond/branch_1_fun/all_to_all | solution.py:268
  109.0 7.2 %local.3 = (bf16[1024,128]{1,0:T(8,128)(2,1)}, bf16[1024,128]{1,0:T(8,128)(2,1)S(1)}, f32[2,1024,128]{2,1,0:T(8,128)S(1)}, bf16[2,1024,128]{2,1,0:T(8,128)(2,1)S(1)}) custom-call(s32[1]{0:T(128)} %bitcast.2.index_ref, bf16[3,1024,128]{2,1,0:T(8,128)(2,1)S(1)} %copy-done.2, bf16[1024,128]{1,0:T(8,128)(2,1)} %get-tuple-element.38.grad_ref, ...), custom_call_target="tpu_custom_call" | custom-call | tf_op jit(solution)/shard_map/cond/branch_1_fun/local/pallas_call | solution.py:240
  116.2 1.3 collective-permute-start.3
  117.4 68.4 %collective-permute-done.3 = bf16[2,1024,128]{2,1,0:T(8,128)(2,1)S(1)} collective-permute-done((bf16[2,1024,128]{2,1,0:T(8,128)(2,1)S(1)}, bf16[2,1024,128]{2,1,0:T(8,128)(2,1)S(1)}, u32[]{:S(2)}, u32[]{:S(2)}) %collective-permute-start.3) | collective-permute-done | bytes 524320 | tf_op jit(solution)/shard_map/cond/branch_1_fun/ppermute | solution.py:262
  185.8 0.1 add_convert_fusion.1
  185.9 0.9 pad_maximum_fusion.1
  186.9 0.0 all-to-all-done.3.returned_ref
  186.9 2.8 %unroute.3 = (bf16[1024,128]{1,0:T(8,128)(2,1)}, bf16[3,1024,128]{2,1,0:T(8,128)(2,1)}) custom-call(bf16[16,96,512]{2,1,0:T(8,128)(2,1)S(1)} %all-to-all-done.3.returned_ref, s32[1024,128]{1,0:T(8,128)S(1)} %get-tuple-element.50.target_ref), custom_call_target="tpu_custom_call" | custom-call | tf_op jit(solution)/shard_map/cond/branch_1_fun/unroute/pallas_call | solution.py:184
Async XLA Ops:
  6.2 15.3 %copy-start.2 = (bf16[3,1024,128]{2,1,0:T(8,128)(2,1)S(1)}, bf16[3,1024,128]{2,1,0:T(8,128)(2,1)}, u32[]{:S(2)}) copy-start(bf16[3,1024,128]{2,1,0:T(8,128)(2,1)} %get-tuple-element.37.qkv_ref) | copy-start | bytes 2359300 | tf_op jit(solution)/shard_map/cond
  6.3 76.2 %all-to-all-start.2 = ((bf16[16,96,512]{2,1,0:T(8,128)(2,1)}), bf16[16,96,512]{2,1,0:T(8,128)(2,1)S(1)}, u32[]{:S(2)}, u32[]{:S(2)}) async-start(bf16[16,96,512]{2,1,0:T(8,128)(2,1)} %get-tuple-element.42), calls=%async_computation.2 | async-start | bytes 3145728 | tf_op jit(solution)/shard_map/cond/branch_1_fun/all_to_all | solution.py:268
  22.4 73.7 %collective-permute-start.2 = (bf16[2,1024,128]{2,1,0:T(8,128)(2,1)}, bf16[2,1024,128]{2,1,0:T(8,128)(2,1)S(1)}, u32[]{:S(2)}, u32[]{:S(2)}) collective-permute-start(bf16[2,1024,128]{2,1,0:T(8,128)(2,1)} %slice.5), channel_id=1, source_target_pairs={{0,32},{32,64},{64,96},{96,128},{128,160},{160,192},{192,224},{224... | collective-permute-start | bytes 1572872 | tf_op jit(solution)/shard_map/cond/branch_1_fun/ppermute | solution.py:262
  96.1 90.8 %all-to-all-start.3 = ((bf16[16,96,512]{2,1,0:T(8,128)(2,1)}), bf16[16,96,512]{2,1,0:T(8,128)(2,1)S(1)}, u32[]{:S(2)}, u32[]{:S(2)}) async-start(bf16[16,96,512]{2,1,0:T(8,128)(2,1)} %cluster.3), calls=%async_computation.3 | async-start | bytes 3145728 | tf_op jit(solution)/shard_map/cond/branch_1_fun/all_to_all | solution.py:268
  116.2 69.7 %collective-permute-start.3 = (bf16[2,1024,128]{2,1,0:T(8,128)(2,1)S(1)}, bf16[2,1024,128]{2,1,0:T(8,128)(2,1)S(1)}, u32[]{:S(2)}, u32[]{:S(2)}) collective-permute-start(bf16[2,1024,128]{2,1,0:T(8,128)(2,1)S(1)} %get-tuple-element.48), channel_id=1, source_target_pairs={{32,0},{64,32},{96,64},{128,96},{160,128},{192,160},{224,192},{256... | collective-permute-start | bytes 1572872 | tf_op jit(solution)/shard_map/cond/branch_1_fun/ppermute | solution.py:262

commit v3 on v2

--- a/solution.py
+++ b/solution.py
@@ -40,9 +40,17 @@
     return output, dquery, dscores, weights
 
 
-def route_kernel(labels_ref, qkv_ref, grad_ref, buffer_ref, target_ref):
+def route_kernel(
+    labels_ref, qkv_hbm, grad_hbm, buffer_hbm, target_hbm, qkv_ref, grad_ref, buffer_ref, target_ref, sems
+):
     tokens = labels_ref.shape[1]
     clusters = buffer_ref.shape[0]
+    loads = [
+        pltpu.make_async_copy(qkv_hbm, qkv_ref, sems.at[0]),
+        pltpu.make_async_copy(grad_hbm, grad_ref, sems.at[1]),
+    ]
+    for load in loads:
+        load.start()
     labels = labels_ref[...]
     block = 256
     lower = lax.broadcasted_iota(jnp.int32, (block, block), 0)
@@ -62,6 +70,10 @@
     target_ref[...] = jnp.transpose(
         jnp.broadcast_to(target.astype(jnp.float32), (128, tokens))
     ).astype(jnp.int32)
+    stores = [pltpu.make_async_copy(target_ref, target_hbm, sems.at[2])]
+    stores[0].start()
+    for load in loads:
+        load.wait()
     payload = jnp.concatenate([qkv_ref[0], qkv_ref[1], qkv_ref[2], grad_ref[...]], axis=1)
     head_size = grad_ref.shape[1]
     slot_rows = lax.broadcasted_iota(jnp.int32, (SLOTS, tokens), 0)
@@ -73,22 +85,41 @@
         first = jnp.where(fill_rows < count, rows[:, :head_size], EMPTY)
         buffer_ref[cluster, :, :head_size] = first.astype(jnp.bfloat16)
         buffer_ref[cluster, :, head_size:] = rows[:, head_size:].astype(jnp.bfloat16)
+        store = pltpu.make_async_copy(
+            buffer_ref.at[cluster], buffer_hbm.at[cluster], sems.at[3 + cluster]
+        )
+        store.start()
+        stores.append(store)
+    for store in stores:
+        store.wait()
 
 
 def route(labels, qkv, grad, clusters):
     tokens, head_size = grad.shape
+    kept = pl.BlockSpec(memory_space=pl.ANY)
     return pl.pallas_call(
         route_kernel,
         out_shape=(
             jax.ShapeDtypeStruct((clusters, SLOTS, 4 * head_size), jnp.bfloat16),
             jax.ShapeDtypeStruct((tokens, 128), jnp.int32),
         ),
+        in_specs=[pl.BlockSpec(memory_space=pltpu.VMEM), kept, kept],
+        out_specs=(kept, kept),
+        scratch_shapes=[
+            pltpu.VMEM(qkv.shape, qkv.dtype),
+            pltpu.VMEM(grad.shape, grad.dtype),
+            pltpu.VMEM((clusters, SLOTS, 4 * head_size), jnp.bfloat16),
+            pltpu.VMEM((tokens, 128), jnp.int32),
+            pltpu.SemaphoreType.DMA((3 + clusters,)),
+        ],
         compiler_params=pltpu.CompilerParams(vmem_limit_bytes=20 << 20),
         name="route",
     )(labels, qkv, grad)
 
 
-def cluster_kernel(received_ref, result_ref, counts_vmem, counts_smem, rows_ref, out_ref, sem):
+def cluster_kernel(
+    received_ref, result_hbm, counts_vmem, counts_smem, rows_ref, out_ref, result_ref, sem, sems
+):
     sources = received_ref.shape[0]
     head_size = received_ref.shape[2] // 4
     tokens = rows_ref.shape[1] - SLOTS
@@ -127,12 +158,20 @@
     out_ref[2, :tokens, :] = key_grad * factor
     out_ref[3, :tokens, :] = value_grad
     out_ref[:, tokens:, :] = jnp.zeros((4, SLOTS, head_size), jnp.float32)
+    stores = []
     for source in range(sources):
         for part in range(4):
             lanes = slice(part * head_size, (part + 1) * head_size)
             result_ref[source, :, lanes] = out_ref[part, pl.ds(starts[source], SLOTS), :].astype(
                 jnp.bfloat16
             )
+        store = pltpu.make_async_copy(
+            result_ref.at[source], result_hbm.at[source], sems.at[source]
+        )
+        store.start()
+        stores.append(store)
+    for store in stores:
+        store.wait()
 
 
 def cluster_attention(received, tokens):
@@ -142,26 +181,31 @@
         cluster_kernel,
         out_shape=jax.ShapeDtypeStruct(received.shape, jnp.bfloat16),
         in_specs=[vmem],
-        out_specs=vmem,
+        out_specs=pl.BlockSpec(memory_space=pl.ANY),
         scratch_shapes=[
             pltpu.VMEM((sources, 128), jnp.int32),
             pltpu.SMEM((sources, 128), jnp.int32),
             pltpu.VMEM((4, tokens + SLOTS, width // 4), jnp.float32),
             pltpu.VMEM((4, tokens + SLOTS, width // 4), jnp.float32),
+            pltpu.VMEM(received.shape, jnp.bfloat16),
             pltpu.SemaphoreType.DMA,
+            pltpu.SemaphoreType.DMA((sources,)),
         ],
         compiler_params=pltpu.CompilerParams(vmem_limit_bytes=28 << 20),
         name="cluster",
     )(received)
 
 
-def unroute_kernel(returned_ref, target_ref, output_ref, grads_ref):
+def unroute_kernel(
+    returned_ref, target_ref, output_hbm, grads_hbm, output_ref, grads_ref, sems
+):
     clusters = returned_ref.shape[0]
     tokens, head_size = output_ref.shape
     slots = clusters * SLOTS
     rows = returned_ref[...].reshape(slots, 4 * head_size)
     block = 256
     lanes = lax.broadcasted_iota(jnp.int32, (block, 128), 1)
+    stores = []
     for row in range(0, tokens, block):
         target = target_ref[row : row + block, :]
         select = jnp.concatenate(
@@ -177,6 +221,16 @@
             grads_ref[part, row : row + block, :] = picked[
                 :, (part + 1) * head_size : (part + 2) * head_size
             ]
+        span = pl.ds(row, block)
+        step = row // block
+        for store in (
+            pltpu.make_async_copy(output_ref.at[span], output_hbm.at[span], sems.at[0, step]),
+            pltpu.make_async_copy(grads_ref.at[:, span], grads_hbm.at[:, span], sems.at[1, step]),
+        ):
+            store.start()
+            stores.append(store)
+    for store in stores:
+        store.wait()
 
 
 def unroute(returned, target, head_size):
@@ -188,6 +242,12 @@
             jax.ShapeDtypeStruct((3, tokens, head_size), jnp.bfloat16),
         ),
         in_specs=[pl.BlockSpec(memory_space=pltpu.VMEM)] * 2,
+        out_specs=(pl.BlockSpec(memory_space=pl.ANY),) * 2,
+        scratch_shapes=[
+            pltpu.VMEM((tokens, head_size), jnp.bfloat16),
+            pltpu.VMEM((3, tokens, head_size), jnp.bfloat16),
+            pltpu.SemaphoreType.DMA((2, 4)),
+        ],
         compiler_params=pltpu.CompilerParams(vmem_limit_bytes=20 << 20),
         name="unroute",
     )(returned, target)
@@ -288,8 +348,9 @@
 
 def local_first(local_qkv, local_grad, routed_qkv, routed_grad, cluster_ids):
     tokens, head_size = local_grad.shape
-    prev = shifted(local_qkv[1:], 1)
     buffer, target = route(cluster_ids, routed_qkv, routed_grad, lax.axis_size("seq"))
+    halo, buffer = lax.optimization_barrier((local_qkv[1:], buffer))
+    prev = shifted(halo, 1)
     index = lax.axis_index("seq").astype(jnp.int32).reshape(1)
     local_out, dquery, own, late = local_attention(index, local_qkv, local_grad, prev)
     buffer, late = lax.optimization_barrier((buffer, late))

time: 190 us -> 190 us (level)
  starting transfers between devices: 33.3 us -> 36.3 us
  waiting for transfers between devices: 131 us -> 128 us
    all_to_all x2, waiting for transfers between devices: 56.2 us -> 50.9 us  [exchange(): return lax.all_to_all(block, 'seq', split_axis=0, concat_axis=0, tiled=True)]
    all_to_all x2, starting transfers between devices: 28.2 us -> 31.1 us  [exchange(): return lax.all_to_all(block, 'seq', split_axis=0, concat_axis=0, tiled=True)]
    ppermute x2, waiting for transfers between devices: 74.6 us -> 77 us  [shifted(): lax.ppermute(block, 'seq', [(i - distance, i) for i in devices if i - dis...]
where the time goes in v3:
time: 190 us
  waiting for transfers between devices  128 us (67%)
  starting transfers between devices  36.3 us (19%)
  Pallas kernels  22.5 us (12%)
    ppermute x2, waiting for transfers between devices, shifted(): lax.ppermute(block, 'seq', [(i - distance, i) for i in devices if i - dis...  77 us
    all_to_all x2, waiting for transfers between devices, exchange(): return lax.all_to_all(block, 'seq', split_axis=0, concat_axis=0, tiled=True)  50.9 us
    all_to_all x2, starting transfers between devices, exchange(): return lax.all_to_all(block, 'seq', split_axis=0, concat_axis=0, tiled=True)  31.1 us
    pallas_call x1, Pallas kernels, cluster_attention(): pl.pallas_call(cluster_kernel, out_shape=jax.ShapeDtypeStruct(received.sh...  7.31 us
    pallas_call x1, Pallas kernels, local_attention(): pl.pallas_call(local_kernel, out_shape=(jax.ShapeDtypeStruct((tokens, hea...  7.2 us
    pallas_call x1, Pallas kernels, route(): pl.pallas_call(route_kernel, out_shape=(jax.ShapeDtypeStruct((clusters, S...  5.47 us
    ppermute x2, starting transfers between devices, shifted(): lax.ppermute(block, 'seq', [(i - distance, i) for i in devices if i - dis...  5.13 us
  transfers between devices with their start and end apart: 4, of which 3 were waited for; matrix products, arithmetic and copies ran while one was open for 1% of the time, Pallas kernels for 8%

profile of v3, /device:TPU:24, one launch (start us, length us, event | category | flops | bytes accessed | tf_op | source)
XLA Modules:
  0.0 190.1 jit_solution(2071485546286266731)
XLA Ops:
  0.6 189.2 %conditional.1 = (bf16[1024,128]{1,0:T(8,128)(2,1)}, bf16[1024,128]{1,0:T(8,128)(2,1)}, bf16[3,1024,128]{2,1,0:T(8,128)(2,1)}, bf16[3,1024,128]{2,1,0:T(8,128)(2,1)}) conditional(s32[]{:T(128)} %convert_element_type.15, (bf16[3,1024,128]{2,1,0:T(8,128)(2,1)}, s32[1,1024]{1,0:T(1,128)}, bf16[3,1024,128]{2,1,0:T(8,128)(2,1)}, ...), branch_computations={%region_0.0_spmd, %region_1.0_spmd} | conditional | flops 1179651 | bytes 24641828 | solution.py:369
  0.9 5.5 %route.3 = (bf16[16,96,512]{2,1,0:T(8,128)(2,1)}, s32[1024,128]{1,0:T(8,128)S(1)}) custom-call(s32[1,1024]{1,0:T(1,128)} %get-tuple-element.41.labels_ref, bf16[3,1024,128]{2,1,0:T(8,128)(2,1)} %get-tuple-element.42.qkv_hbm, bf16[1024,128]{1,0:T(8,128)(2,1)} %get-tuple-element.43.grad_hbm), custom_call_target="tpu_custom_call" | custom-call | tf_op jit(solution)/shard_map/cond/branch_1_fun/route/pallas_call | solution.py:100
  6.4 0.0 copy-start.2
  6.4 15.3 %all-to-all-start.2 = ((bf16[16,96,512]{2,1,0:T(8,128)(2,1)}), bf16[16,96,512]{2,1,0:T(8,128)(2,1)S(1)}, u32[]{:S(2)}, u32[]{:S(2)}) async-start(bf16[16,96,512]{2,1,0:T(8,128)(2,1)} %get-tuple-element.44), calls=%async_computation.2 | async-start | bytes 3145728 | tf_op jit(solution)/shard_map/cond/branch_1_fun/all_to_all | solution.py:328
  21.7 0.0 copy-done.2
  21.7 0.8 slice.5
  22.6 3.8 %collective-permute-start.2 = (bf16[2,1024,128]{2,1,0:T(8,128)(2,1)}, bf16[2,1024,128]{2,1,0:T(8,128)(2,1)S(1)}, u32[]{:S(2)}, u32[]{:S(2)}) collective-permute-start(bf16[2,1024,128]{2,1,0:T(8,128)(2,1)} %slice.5), channel_id=1, source_target_pairs={{0,32},{32,64},{64,96},{96,128},{128,160},{160,192},{192,224},{224... | collective-permute-start | bytes 1572872 | tf_op jit(solution)/shard_map/cond/branch_1_fun/ppermute | solution.py:322
  26.4 50.9 %all-to-all-done.2.received_ref = bf16[16,96,512]{2,1,0:T(8,128)(2,1)S(1)} async-done(((bf16[16,96,512]{2,1,0:T(8,128)(2,1)}), bf16[16,96,512]{2,1,0:T(8,128)(2,1)S(1)}, u32[]{:S(2)}, u32[]{:S(2)}) %all-to-all-start.2) | async-done | bytes 1572896 | tf_op jit(solution)/shard_map/cond/branch_1_fun/all_to_all | solution.py:328
  77.3 7.3 %cluster.3 = bf16[16,96,512]{2,1,0:T(8,128)(2,1)} custom-call(bf16[16,96,512]{2,1,0:T(8,128)(2,1)S(1)} %all-to-all-done.2.received_ref), custom_call_target="tpu_custom_call" | custom-call | tf_op jit(solution)/shard_map/cond/branch_1_fun/cluster/pallas_call | solution.py:180
  84.7 8.6 %collective-permute-done.2.prev_ref = bf16[2,1024,128]{2,1,0:T(8,128)(2,1)S(1)} collective-permute-done((bf16[2,1024,128]{2,1,0:T(8,128)(2,1)}, bf16[2,1024,128]{2,1,0:T(8,128)(2,1)S(1)}, u32[]{:S(2)}, u32[]{:S(2)}) %collective-permute-start.2) | collective-permute-done | bytes 524320 | tf_op jit(solution)/shard_map/cond/branch_1_fun/ppermute | solution.py:322
  93.3 15.8 %all-to-all-start.3 = ((bf16[16,96,512]{2,1,0:T(8,128)(2,1)}), bf16[16,96,512]{2,1,0:T(8,128)(2,1)S(1)}, u32[]{:S(2)}, u32[]{:S(2)}) async-start(bf16[16,96,512]{2,1,0:T(8,128)(2,1)} %cluster.3), calls=%async_computation.3 | async-start | bytes 3145728 | tf_op jit(solution)/shard_map/cond/branch_1_fun/all_to_all | solution.py:328
  109.1 7.2 %local.3 = (bf16[1024,128]{1,0:T(8,128)(2,1)}, bf16[1024,128]{1,0:T(8,128)(2,1)S(1)}, f32[2,1024,128]{2,1,0:T(8,128)S(1)}, bf16[2,1024,128]{2,1,0:T(8,128)(2,1)S(1)}) custom-call(s32[1]{0:T(128)} %bitcast.2.index_ref, bf16[3,1024,128]{2,1,0:T(8,128)(2,1)S(1)} %copy-done.2, bf16[1024,128]{1,0:T(8,128)(2,1)} %get-tuple-element.40.grad_ref, ...), custom_call_target="tpu_custom_call" | custom-call | tf_op jit(solution)/shard_map/cond/branch_1_fun/local/pallas_call | solution.py:300
  116.3 1.3 collective-permute-start.3
  117.6 68.4 %collective-permute-done.3 = bf16[2,1024,128]{2,1,0:T(8,128)(2,1)S(1)} collective-permute-done((bf16[2,1024,128]{2,1,0:T(8,128)(2,1)S(1)}, bf16[2,1024,128]{2,1,0:T(8,128)(2,1)S(1)}, u32[]{:S(2)}, u32[]{:S(2)}) %collective-permute-start.3) | collective-permute-done | bytes 524320 | tf_op jit(solution)/shard_map/cond/branch_1_fun/ppermute | solution.py:322
  186.0 0.1 add_convert_fusion.1
  186.1 0.9 pad_maximum_fusion.1
  187.0 0.0 all-to-all-done.3.returned_ref
  187.0 2.6 %unroute.3 = (bf16[1024,128]{1,0:T(8,128)(2,1)}, bf16[3,1024,128]{2,1,0:T(8,128)(2,1)}) custom-call(bf16[16,96,512]{2,1,0:T(8,128)(2,1)S(1)} %all-to-all-done.3.returned_ref, s32[1024,128]{1,0:T(8,128)S(1)} %get-tuple-element.52.target_ref), custom_call_target="tpu_custom_call" | custom-call | tf_op jit(solution)/shard_map/cond/branch_1_fun/unroute/pallas_call | solution.py:238
Async XLA Ops:
  6.4 15.4 %copy-start.2 = (bf16[3,1024,128]{2,1,0:T(8,128)(2,1)S(1)}, bf16[3,1024,128]{2,1,0:T(8,128)(2,1)}, u32[]{:S(2)}) copy-start(bf16[3,1024,128]{2,1,0:T(8,128)(2,1)} %get-tuple-element.39.qkv_ref) | copy-start | bytes 2359300 | tf_op jit(solution)/shard_map/cond
  6.4 71.0 %all-to-all-start.2 = ((bf16[16,96,512]{2,1,0:T(8,128)(2,1)}), bf16[16,96,512]{2,1,0:T(8,128)(2,1)S(1)}, u32[]{:S(2)}, u32[]{:S(2)}) async-start(bf16[16,96,512]{2,1,0:T(8,128)(2,1)} %get-tuple-element.44), calls=%async_computation.2 | async-start | bytes 3145728 | tf_op jit(solution)/shard_map/cond/branch_1_fun/all_to_all | solution.py:328
  22.6 70.7 %collective-permute-start.2 = (bf16[2,1024,128]{2,1,0:T(8,128)(2,1)}, bf16[2,1024,128]{2,1,0:T(8,128)(2,1)S(1)}, u32[]{:S(2)}, u32[]{:S(2)}) collective-permute-start(bf16[2,1024,128]{2,1,0:T(8,128)(2,1)} %slice.5), channel_id=1, source_target_pairs={{0,32},{32,64},{64,96},{96,128},{128,160},{160,192},{192,224},{224... | collective-permute-start | bytes 1572872 | tf_op jit(solution)/shard_map/cond/branch_1_fun/ppermute | solution.py:322
  93.3 93.7 %all-to-all-start.3 = ((bf16[16,96,512]{2,1,0:T(8,128)(2,1)}), bf16[16,96,512]{2,1,0:T(8,128)(2,1)S(1)}, u32[]{:S(2)}, u32[]{:S(2)}) async-start(bf16[16,96,512]{2,1,0:T(8,128)(2,1)} %cluster.3), calls=%async_computation.3 | async-start | bytes 3145728 | tf_op jit(solution)/shard_map/cond/branch_1_fun/all_to_all | solution.py:328
  116.3 69.7 %collective-permute-start.3 = (bf16[2,1024,128]{2,1,0:T(8,128)(2,1)S(1)}, bf16[2,1024,128]{2,1,0:T(8,128)(2,1)S(1)}, u32[]{:S(2)}, u32[]{:S(2)}) collective-permute-start(bf16[2,1024,128]{2,1,0:T(8,128)(2,1)S(1)} %get-tuple-element.50), channel_id=1, source_target_pairs={{32,0},{64,32},{96,64},{128,96},{160,128},{192,160},{224,192},{256... | collective-permute-start | bytes 1572872 | tf_op jit(solution)/shard_map/cond/branch_1_fun/ppermute | solution.py:322

commit v4 on v3

--- a/solution.py
+++ b/solution.py
@@ -9,6 +9,8 @@
 SLOTS = 96
 EMPTY = 512.0
 masked_fill = -1e30
+LOCAL_FLOPS = 10 * 1024 * 1280 * 128
+HIDDEN_FLOPS = 200 * 10**9
 
 
 def dot_nn(a, b):
@@ -294,7 +296,7 @@
     own_ref[1] = value_acc[tokens:, :]
 
 
-def local_attention(index, qkv, grad, prev):
+def local_attention(index, qkv, grad, prev, cost):
     tokens, head_size = grad.shape
     vmem = pl.BlockSpec(memory_space=pltpu.VMEM)
     return pl.pallas_call(
@@ -313,6 +315,9 @@
             pltpu.VMEM((2 * tokens, head_size), jnp.float32),
         ],
         compiler_params=pltpu.CompilerParams(vmem_limit_bytes=28 << 20),
+        cost_estimate=pl.CostEstimate(
+            flops=cost, transcendentals=tokens * (WIN + 256), bytes_accessed=12 * tokens * head_size
+        ),
         name="local",
     )(index, qkv, grad, prev)
 
@@ -335,10 +340,11 @@
     halo, buffer = lax.optimization_barrier((local_qkv[1:], buffer))
     prev = shifted(halo, 1)
     result = cluster_attention(received, tokens)
-    result, prev = lax.optimization_barrier((result, prev))
     returned = exchange(result)
     index = lax.axis_index("seq").astype(jnp.int32).reshape(1)
-    local_out, dquery, own, late = local_attention(index, local_qkv, local_grad, prev)
+    local_out, dquery, own, late = local_attention(
+        index, local_qkv, local_grad, prev, HIDDEN_FLOPS
+    )
     late = shifted(late, -1)
     joined = (own + late.astype(jnp.float32)).astype(jnp.bfloat16)
     local_dqkv = jnp.concatenate([dquery[None], joined], axis=0)
@@ -352,7 +358,9 @@
     halo, buffer = lax.optimization_barrier((local_qkv[1:], buffer))
     prev = shifted(halo, 1)
     index = lax.axis_index("seq").astype(jnp.int32).reshape(1)
-    local_out, dquery, own, late = local_attention(index, local_qkv, local_grad, prev)
+    local_out, dquery, own, late = local_attention(
+        index, local_qkv, local_grad, prev, LOCAL_FLOPS
+    )
     buffer, late = lax.optimization_barrier((buffer, late))
     received = exchange(buffer)
     late = shifted(late, -1)

time: 190 us -> 188 us (0.989)
  waiting for transfers between devices: 128 us -> 120 us
  starting transfers between devices: 36.3 us -> 41.2 us
    ppermute x2, waiting for transfers between devices: 77 us -> 69.3 us  [shifted(): lax.ppermute(block, 'seq', [(i - distance, i) for i in devices if i - dis...]
    all_to_all x2, starting transfers between devices: 31.1 us -> 36.1 us  [exchange(): return lax.all_to_all(block, 'seq', split_axis=0, concat_axis=0, tiled=True)]
  transfers between devices with their start and end apart: 4 -> 4, of which waited for: 3 -> 2; matrix products, arithmetic and copies ran while one was open for 1% -> 1% of each run, Pallas kernels for 8% -> 7%
where the time goes in v4:
time: 188 us
  waiting for transfers between devices  120 us (64%)
  starting transfers between devices  41.2 us (22%)
  Pallas kernels  23 us (12%)
    ppermute x2, waiting for transfers between devices, shifted(): lax.ppermute(block, 'seq', [(i - distance, i) for i in devices if i - dis...  69.3 us
    all_to_all x2, waiting for transfers between devices, exchange(): return lax.all_to_all(block, 'seq', split_axis=0, concat_axis=0, tiled=True)  50.9 us
    all_to_all x2, starting transfers between devices, exchange(): return lax.all_to_all(block, 'seq', split_axis=0, concat_axis=0, tiled=True)  36.1 us
    pallas_call x1, Pallas kernels, cluster_attention(): pl.pallas_call(cluster_kernel, out_shape=jax.ShapeDtypeStruct(received.sh...  7.3 us
    pallas_call x1, Pallas kernels, local_attention(): pl.pallas_call(local_kernel, out_shape=(jax.ShapeDtypeStruct((tokens, hea...  6.24 us
    pallas_call x1, Pallas kernels, route(): pl.pallas_call(route_kernel, out_shape=(jax.ShapeDtypeStruct((clusters, S...  5.48 us
    ppermute x2, starting transfers between devices, shifted(): lax.ppermute(block, 'seq', [(i - distance, i) for i in devices if i - dis...  5.13 us
    pallas_call x1, Pallas kernels, unroute(): pl.pallas_call(unroute_kernel, out_shape=(jax.ShapeDtypeStruct((tokens, h...  3.97 us
  transfers between devices with their start and end apart: 4, of which 2 were waited for; matrix products, arithmetic and copies ran while one was open for 1% of the time, Pallas kernels for 7%

profile of v4, /device:TPU:24, one launch (start us, length us, event | category | flops | bytes accessed | tf_op | source)
XLA Modules:
  0.0 187.5 jit_solution(16584357804086852695)
XLA Ops:
  0.6 186.0 %conditional.1 = (bf16[1024,128]{1,0:T(8,128)(2,1)}, bf16[1024,128]{1,0:T(8,128)(2,1)}, bf16[3,1024,128]{2,1,0:T(8,128)(2,1)}, bf16[3,1024,128]{2,1,0:T(8,128)(2,1)S(1)}) conditional(s32[]{:T(128)} %convert_element_type.15, (bf16[3,1024,128]{2,1,0:T(8,128)(2,1)}, s32[1,1024]{1,0:T(1,128)}, bf16[3,1024,128]{2,1,0:T(8,128)(2,1)}, ...), branch_computations={%region_0.0_spmd, %region_1.0_spmd} | conditional | flops 200001175552 | bytes 29360448 | solution.py:377
  0.9 5.5 %route.3 = (bf16[16,96,512]{2,1,0:T(8,128)(2,1)}, s32[1024,128]{1,0:T(8,128)S(1)}) custom-call(s32[1,1024]{1,0:T(1,128)} %get-tuple-element.41.labels_ref, bf16[3,1024,128]{2,1,0:T(8,128)(2,1)} %get-tuple-element.42.qkv_hbm, bf16[1024,128]{1,0:T(8,128)(2,1)} %get-tuple-element.43.grad_hbm), custom_call_target="tpu_custom_call" | custom-call | tf_op jit(solution)/shard_map/cond/branch_1_fun/route/pallas_call | solution.py:102
  6.4 0.0 copy-start.3
  6.4 15.3 %all-to-all-start.2 = ((bf16[16,96,512]{2,1,0:T(8,128)(2,1)}), bf16[16,96,512]{2,1,0:T(8,128)(2,1)S(1)}, u32[]{:S(2)}, u32[]{:S(2)}) async-start(bf16[16,96,512]{2,1,0:T(8,128)(2,1)} %get-tuple-element.44), calls=%async_computation.2 | async-start | bytes 3145728 | tf_op jit(solution)/shard_map/cond/branch_1_fun/all_to_all | solution.py:333
  21.7 0.0 copy-done.3
  21.7 0.8 slice.5
  22.6 3.8 %collective-permute-start.2 = (bf16[2,1024,128]{2,1,0:T(8,128)(2,1)}, bf16[2,1024,128]{2,1,0:T(8,128)(2,1)S(1)}, u32[]{:S(2)}, u32[]{:S(2)}) collective-permute-start(bf16[2,1024,128]{2,1,0:T(8,128)(2,1)} %slice.5), channel_id=1, source_target_pairs={{0,32},{32,64},{64,96},{96,128},{128,160},{160,192},{192,224},{224... | collective-permute-start | bytes 1572872 | tf_op jit(solution)/shard_map/cond/branch_1_fun/ppermute | solution.py:327
  26.4 50.9 %all-to-all-done.2.received_ref = bf16[16,96,512]{2,1,0:T(8,128)(2,1)S(1)} async-done(((bf16[16,96,512]{2,1,0:T(8,128)(2,1)}), bf16[16,96,512]{2,1,0:T(8,128)(2,1)S(1)}, u32[]{:S(2)}, u32[]{:S(2)}) %all-to-all-start.2) | async-done | bytes 1572896 | tf_op jit(solution)/shard_map/cond/branch_1_fun/all_to_all | solution.py:333
  77.3 7.3 %cluster.3 = bf16[16,96,512]{2,1,0:T(8,128)(2,1)} custom-call(bf16[16,96,512]{2,1,0:T(8,128)(2,1)S(1)} %all-to-all-done.2.received_ref), custom_call_target="tpu_custom_call" | custom-call | tf_op jit(solution)/shard_map/cond/branch_1_fun/cluster/pallas_call | solution.py:182
  84.6 0.0 copy-start.6
  84.6 20.7 %all-to-all-start.3 = ((bf16[16,96,512]{2,1,0:T(8,128)(2,1)}), bf16[16,96,512]{2,1,0:T(8,128)(2,1)}, u32[]{:S(2)}, u32[]{:S(2)}) async-start(bf16[16,96,512]{2,1,0:T(8,128)(2,1)} %cluster.3), calls=%async_computation.3 | async-start | bytes 3145728 | tf_op jit(solution)/shard_map/cond/branch_1_fun/all_to_all | solution.py:333
  105.3 0.0 collective-permute-done.2.prev_ref
  105.4 0.0 copy-done.6
  105.4 6.2 %local.3 = (bf16[1024,128]{1,0:T(8,128)(2,1)}, bf16[1024,128]{1,0:T(8,128)(2,1)S(1)}, f32[2,1024,128]{2,1,0:T(8,128)S(1)}, bf16[2,1024,128]{2,1,0:T(8,128)(2,1)S(1)}) custom-call(s32[1]{0:T(128)} %bitcast.2.index_ref, bf16[3,1024,128]{2,1,0:T(8,128)(2,1)S(1)} %copy-done.3, bf16[1024,128]{1,0:T(8,128)(2,1)S(1)} %copy-done.6, ...), custom_call_target="tpu_custom_call" | custom-call | flops 199999995904 | bytes 1572864 | tf_op jit(solution)/shard_map/cond/branch_1_fun/local/pallas_call | solution.py:302
  111.6 1.3 collective-permute-start.3
  112.9 69.3 %collective-permute-done.3 = bf16[2,1024,128]{2,1,0:T(8,128)(2,1)S(1)} collective-permute-done((bf16[2,1024,128]{2,1,0:T(8,128)(2,1)S(1)}, bf16[2,1024,128]{2,1,0:T(8,128)(2,1)S(1)}, u32[]{:S(2)}, u32[]{:S(2)}) %collective-permute-start.3) | collective-permute-done | bytes 524320 | tf_op jit(solution)/shard_map/cond/branch_1_fun/ppermute | solution.py:327
  182.2 0.1 add_convert_fusion.1
  182.3 0.1 pad_maximum_fusion.1
  182.3 0.0 all-to-all-done.3.returned_ref
  182.4 4.0 %unroute.3 = (bf16[1024,128]{1,0:T(8,128)(2,1)}, bf16[3,1024,128]{2,1,0:T(8,128)(2,1)}) custom-call(bf16[16,96,512]{2,1,0:T(8,128)(2,1)} %all-to-all-done.3.returned_ref, s32[1024,128]{1,0:T(8,128)S(1)} %get-tuple-element.50.target_ref), custom_call_target="tpu_custom_call" | custom-call | tf_op jit(solution)/shard_map/cond/branch_1_fun/unroute/pallas_call | solution.py:240
  186.6 0.0 copy-start.4
  186.6 0.9 copy-done.4
Async XLA Ops:
  6.4 15.4 %copy-start.3 = (bf16[3,1024,128]{2,1,0:T(8,128)(2,1)S(1)}, bf16[3,1024,128]{2,1,0:T(8,128)(2,1)}, u32[]{:S(2)}) copy-start(bf16[3,1024,128]{2,1,0:T(8,128)(2,1)} %get-tuple-element.39.qkv_ref) | copy-start | bytes 2359300 | tf_op jit(solution)/shard_map/cond
  6.4 70.9 %all-to-all-start.2 = ((bf16[16,96,512]{2,1,0:T(8,128)(2,1)}), bf16[16,96,512]{2,1,0:T(8,128)(2,1)S(1)}, u32[]{:S(2)}, u32[]{:S(2)}) async-start(bf16[16,96,512]{2,1,0:T(8,128)(2,1)} %get-tuple-element.44), calls=%async_computation.2 | async-start | bytes 3145728 | tf_op jit(solution)/shard_map/cond/branch_1_fun/all_to_all | solution.py:333
  22.6 82.8 %collective-permute-start.2 = (bf16[2,1024,128]{2,1,0:T(8,128)(2,1)}, bf16[2,1024,128]{2,1,0:T(8,128)(2,1)S(1)}, u32[]{:S(2)}, u32[]{:S(2)}) collective-permute-start(bf16[2,1024,128]{2,1,0:T(8,128)(2,1)} %slice.5), channel_id=1, source_target_pairs={{0,32},{32,64},{64,96},{96,128},{128,160},{160,192},{192,224},{224... | collective-permute-start | bytes 1572872 | tf_op jit(solution)/shard_map/cond/branch_1_fun/ppermute | solution.py:327
  84.6 20.8 %copy-start.6 = (bf16[1024,128]{1,0:T(8,128)(2,1)S(1)}, bf16[1024,128]{1,0:T(8,128)(2,1)}, u32[]{:S(2)}) copy-start(bf16[1024,128]{1,0:T(8,128)(2,1)} %get-tuple-element.40.grad_ref) | copy-start | bytes 786436 | tf_op jit(solution)/shard_map/cond
  84.6 97.8 %all-to-all-start.3 = ((bf16[16,96,512]{2,1,0:T(8,128)(2,1)}), bf16[16,96,512]{2,1,0:T(8,128)(2,1)}, u32[]{:S(2)}, u32[]{:S(2)}) async-start(bf16[16,96,512]{2,1,0:T(8,128)(2,1)} %cluster.3), calls=%async_computation.3 | async-start | bytes 3145728 | tf_op jit(solution)/shard_map/cond/branch_1_fun/all_to_all | solution.py:333
  111.6 70.6 %collective-permute-start.3 = (bf16[2,1024,128]{2,1,0:T(8,128)(2,1)S(1)}, bf16[2,1024,128]{2,1,0:T(8,128)(2,1)S(1)}, u32[]{:S(2)}, u32[]{:S(2)}) collective-permute-start(bf16[2,1024,128]{2,1,0:T(8,128)(2,1)S(1)} %get-tuple-element.49), channel_id=1, source_target_pairs={{32,0},{64,32},{96,64},{128,96},{160,128},{192,160},{224,192},{256... | collective-permute-start | bytes 1572872 | tf_op jit(solution)/shard_map/cond/branch_1_fun/ppermute | solution.py:327
  186.6 0.9 copy-start.4

commit v5 on v4

--- a/solution.py
+++ b/solution.py
@@ -43,17 +43,34 @@
 
 
 def route_kernel(
-    labels_ref, qkv_hbm, grad_hbm, buffer_hbm, target_hbm, qkv_ref, grad_ref, buffer_ref, target_ref, sems
+    labels_hbm,
+    qkv_hbm,
+    grad_hbm,
+    buffer_hbm,
+    target_hbm,
+    labels_ref,
+    qkv_ref,
+    grad_ref,
+    buffer_ref,
+    target_ref,
+    sems,
 ):
     tokens = labels_ref.shape[1]
     clusters = buffer_ref.shape[0]
-    loads = [
-        pltpu.make_async_copy(qkv_hbm, qkv_ref, sems.at[0]),
-        pltpu.make_async_copy(grad_hbm, grad_ref, sems.at[1]),
-    ]
+    half = tokens // 2
+    first_load = pltpu.make_async_copy(labels_hbm, labels_ref, sems.at[0])
+    first_load.start()
+    loads = []
+    for part in range(4):
+        for piece in range(2):
+            rows = pl.ds(piece * half, half)
+            if part < 3:
+                pair = (qkv_hbm.at[part, rows], qkv_ref.at[part, rows])
+            else:
+                pair = (grad_hbm.at[rows], grad_ref.at[rows])
+            loads.append(pltpu.make_async_copy(*pair, sems.at[2 + 2 * part + piece]))
     for load in loads:
         load.start()
-    labels = labels_ref[...]
     block = 256
     lower = lax.broadcasted_iota(jnp.int32, (block, block), 0)
     upper = lax.broadcasted_iota(jnp.int32, (block, block), 1)
@@ -61,6 +78,8 @@
     cluster_rows = lax.broadcasted_iota(jnp.int32, (clusters, block), 0)
     running = jnp.zeros((clusters, 1), jnp.float32)
     targets = []
+    first_load.wait()
+    labels = labels_ref[...]
     for start in range(0, tokens, block):
         part = labels[:, start : start + block]
         onehot = (cluster_rows == part).astype(jnp.float32)
@@ -72,7 +91,7 @@
     target_ref[...] = jnp.transpose(
         jnp.broadcast_to(target.astype(jnp.float32), (128, tokens))
     ).astype(jnp.int32)
-    stores = [pltpu.make_async_copy(target_ref, target_hbm, sems.at[2])]
+    stores = [pltpu.make_async_copy(target_ref, target_hbm, sems.at[1])]
     stores[0].start()
     for load in loads:
         load.wait()
@@ -88,7 +107,7 @@
         buffer_ref[cluster, :, :head_size] = first.astype(jnp.bfloat16)
         buffer_ref[cluster, :, head_size:] = rows[:, head_size:].astype(jnp.bfloat16)
         store = pltpu.make_async_copy(
-            buffer_ref.at[cluster], buffer_hbm.at[cluster], sems.at[3 + cluster]
+            buffer_ref.at[cluster], buffer_hbm.at[cluster], sems.at[10 + cluster]
         )
         store.start()
         stores.append(store)
@@ -105,14 +124,15 @@
             jax.ShapeDtypeStruct((clusters, SLOTS, 4 * head_size), jnp.bfloat16),
             jax.ShapeDtypeStruct((tokens, 128), jnp.int32),
         ),
-        in_specs=[pl.BlockSpec(memory_space=pltpu.VMEM), kept, kept],
+        in_specs=[kept, kept, kept],
         out_specs=(kept, kept),
         scratch_shapes=[
+            pltpu.VMEM(labels.shape, labels.dtype),
             pltpu.VMEM(qkv.shape, qkv.dtype),
             pltpu.VMEM(grad.shape, grad.dtype),
             pltpu.VMEM((clusters, SLOTS, 4 * head_size), jnp.bfloat16),
             pltpu.VMEM((tokens, 128), jnp.int32),
-            pltpu.SemaphoreType.DMA((3 + clusters,)),
+            pltpu.SemaphoreType.DMA((10 + clusters,)),
         ],
         compiler_params=pltpu.CompilerParams(vmem_limit_bytes=20 << 20),
         name="route",

time: 188 us -> 187 us (level)
  no operation moved by 1% of the time
where the time goes in v5:
time: 187 us
  waiting for transfers between devices  120 us (64%)
  starting transfers between devices  41.4 us (22%)
  Pallas kernels  22.5 us (12%)
    ppermute x2, waiting for transfers between devices, shifted(): lax.ppermute(block, 'seq', [(i - distance, i) for i in devices if i - dis...  69.3 us
    all_to_all x2, waiting for transfers between devices, exchange(): return lax.all_to_all(block, 'seq', split_axis=0, concat_axis=0, tiled=True)  50.4 us
    all_to_all x2, starting transfers between devices, exchange(): return lax.all_to_all(block, 'seq', split_axis=0, concat_axis=0, tiled=True)  36.3 us
    pallas_call x1, Pallas kernels, cluster_attention(): pl.pallas_call(cluster_kernel, out_shape=jax.ShapeDtypeStruct(received.sh...  7.29 us
    pallas_call x1, Pallas kernels, local_attention(): pl.pallas_call(local_kernel, out_shape=(jax.ShapeDtypeStruct((tokens, hea...  6.24 us
    ppermute x2, starting transfers between devices, shifted(): lax.ppermute(block, 'seq', [(i - distance, i) for i in devices if i - dis...  5.13 us
    pallas_call x1, Pallas kernels, route(): pl.pallas_call(route_kernel, out_shape=(jax.ShapeDtypeStruct((clusters, S...  4.96 us
    pallas_call x1, Pallas kernels, unroute(): pl.pallas_call(unroute_kernel, out_shape=(jax.ShapeDtypeStruct((tokens, h...  3.97 us
  transfers between devices with their start and end apart: 4, of which 2 were waited for; matrix products, arithmetic and copies ran while one was open for 1% of the time, Pallas kernels for 7%

profile of v5, /device:TPU:24, one launch (start us, length us, event | category | flops | bytes accessed | tf_op | source)
XLA Modules:
  0.0 186.8 jit_solution(7762628171792884399)
XLA Ops:
  0.6 185.3 %conditional.1 = (bf16[1024,128]{1,0:T(8,128)(2,1)}, bf16[1024,128]{1,0:T(8,128)(2,1)}, bf16[3,1024,128]{2,1,0:T(8,128)(2,1)}, bf16[3,1024,128]{2,1,0:T(8,128)(2,1)S(1)}) conditional(s32[]{:T(128)} %convert_element_type.15, (bf16[3,1024,128]{2,1,0:T(8,128)(2,1)}, s32[1,1024]{1,0:T(1,128)}, bf16[3,1024,128]{2,1,0:T(8,128)(2,1)}, ...), branch_computations={%region_0.0_spmd, %region_1.0_spmd} | conditional | flops 200001175552 | bytes 29360448 | solution.py:397
  0.9 5.0 %route.3 = (bf16[16,96,512]{2,1,0:T(8,128)(2,1)}, s32[1024,128]{1,0:T(8,128)S(1)}) custom-call(s32[1,1024]{1,0:T(1,128)} %get-tuple-element.41.labels_hbm, bf16[3,1024,128]{2,1,0:T(8,128)(2,1)} %get-tuple-element.42.qkv_hbm, bf16[1024,128]{1,0:T(8,128)(2,1)} %get-tuple-element.43.grad_hbm), custom_call_target="tpu_custom_call" | custom-call | tf_op jit(solution)/shard_map/cond/branch_1_fun/route/pallas_call | solution.py:121
  5.8 0.0 copy-start.3
  5.9 15.3 %all-to-all-start.2 = ((bf16[16,96,512]{2,1,0:T(8,128)(2,1)}), bf16[16,96,512]{2,1,0:T(8,128)(2,1)S(1)}, u32[]{:S(2)}, u32[]{:S(2)}) async-start(bf16[16,96,512]{2,1,0:T(8,128)(2,1)} %get-tuple-element.44), calls=%async_computation.2 | async-start | bytes 3145728 | tf_op jit(solution)/shard_map/cond/branch_1_fun/all_to_all | solution.py:353
  21.2 0.0 copy-done.3
  21.2 0.8 slice.5
  22.0 3.8 %collective-permute-start.2 = (bf16[2,1024,128]{2,1,0:T(8,128)(2,1)}, bf16[2,1024,128]{2,1,0:T(8,128)(2,1)S(1)}, u32[]{:S(2)}, u32[]{:S(2)}) collective-permute-start(bf16[2,1024,128]{2,1,0:T(8,128)(2,1)} %slice.5), channel_id=1, source_target_pairs={{0,32},{32,64},{64,96},{96,128},{128,160},{160,192},{192,224},{224... | collective-permute-start | bytes 1572872 | tf_op jit(solution)/shard_map/cond/branch_1_fun/ppermute | solution.py:347
  25.9 50.4 %all-to-all-done.2.received_ref = bf16[16,96,512]{2,1,0:T(8,128)(2,1)S(1)} async-done(((bf16[16,96,512]{2,1,0:T(8,128)(2,1)}), bf16[16,96,512]{2,1,0:T(8,128)(2,1)S(1)}, u32[]{:S(2)}, u32[]{:S(2)}) %all-to-all-start.2) | async-done | bytes 1572896 | tf_op jit(solution)/shard_map/cond/branch_1_fun/all_to_all | solution.py:353
  76.3 7.3 %cluster.3 = bf16[16,96,512]{2,1,0:T(8,128)(2,1)} custom-call(bf16[16,96,512]{2,1,0:T(8,128)(2,1)S(1)} %all-to-all-done.2.received_ref), custom_call_target="tpu_custom_call" | custom-call | tf_op jit(solution)/shard_map/cond/branch_1_fun/cluster/pallas_call | solution.py:202
  83.6 0.0 copy-start.6
  83.6 21.0 %all-to-all-start.3 = ((bf16[16,96,512]{2,1,0:T(8,128)(2,1)}), bf16[16,96,512]{2,1,0:T(8,128)(2,1)}, u32[]{:S(2)}, u32[]{:S(2)}) async-start(bf16[16,96,512]{2,1,0:T(8,128)(2,1)} %cluster.3), calls=%async_computation.3 | async-start | bytes 3145728 | tf_op jit(solution)/shard_map/cond/branch_1_fun/all_to_all | solution.py:353
  104.6 0.0 collective-permute-done.2.prev_ref
  104.6 0.0 copy-done.6
  104.6 6.2 %local.3 = (bf16[1024,128]{1,0:T(8,128)(2,1)}, bf16[1024,128]{1,0:T(8,128)(2,1)S(1)}, f32[2,1024,128]{2,1,0:T(8,128)S(1)}, bf16[2,1024,128]{2,1,0:T(8,128)(2,1)S(1)}) custom-call(s32[1]{0:T(128)} %bitcast.2.index_ref, bf16[3,1024,128]{2,1,0:T(8,128)(2,1)S(1)} %copy-done.3, bf16[1024,128]{1,0:T(8,128)(2,1)S(1)} %copy-done.6, ...), custom_call_target="tpu_custom_call" | custom-call | flops 199999995904 | bytes 1572864 | tf_op jit(solution)/shard_map/cond/branch_1_fun/local/pallas_call | solution.py:322
  110.9 1.3 collective-permute-start.3
  112.2 69.3 %collective-permute-done.3 = bf16[2,1024,128]{2,1,0:T(8,128)(2,1)S(1)} collective-permute-done((bf16[2,1024,128]{2,1,0:T(8,128)(2,1)S(1)}, bf16[2,1024,128]{2,1,0:T(8,128)(2,1)S(1)}, u32[]{:S(2)}, u32[]{:S(2)}) %collective-permute-start.3) | collective-permute-done | bytes 524320 | tf_op jit(solution)/shard_map/cond/branch_1_fun/ppermute | solution.py:347
  181.4 0.1 add_convert_fusion.1
  181.5 0.1 pad_maximum_fusion.1
  181.6 0.0 all-to-all-done.3.returned_ref
  181.6 4.0 %unroute.3 = (bf16[1024,128]{1,0:T(8,128)(2,1)}, bf16[3,1024,128]{2,1,0:T(8,128)(2,1)}) custom-call(bf16[16,96,512]{2,1,0:T(8,128)(2,1)} %all-to-all-done.3.returned_ref, s32[1024,128]{1,0:T(8,128)S(1)} %get-tuple-element.50.target_ref), custom_call_target="tpu_custom_call" | custom-call | tf_op jit(solution)/shard_map/cond/branch_1_fun/unroute/pallas_call | solution.py:260
  185.9 0.0 copy-start.4
  185.9 0.9 copy-done.4
Async XLA Ops:
  5.8 15.4 %copy-start.3 = (bf16[3,1024,128]{2,1,0:T(8,128)(2,1)S(1)}, bf16[3,1024,128]{2,1,0:T(8,128)(2,1)}, u32[]{:S(2)}) copy-start(bf16[3,1024,128]{2,1,0:T(8,128)(2,1)} %get-tuple-element.39.qkv_ref) | copy-start | bytes 2359300 | tf_op jit(solution)/shard_map/cond
  5.9 70.5 %all-to-all-start.2 = ((bf16[16,96,512]{2,1,0:T(8,128)(2,1)}), bf16[16,96,512]{2,1,0:T(8,128)(2,1)S(1)}, u32[]{:S(2)}, u32[]{:S(2)}) async-start(bf16[16,96,512]{2,1,0:T(8,128)(2,1)} %get-tuple-element.44), calls=%async_computation.2 | async-start | bytes 3145728 | tf_op jit(solution)/shard_map/cond/branch_1_fun/all_to_all | solution.py:353
  22.0 82.6 %collective-permute-start.2 = (bf16[2,1024,128]{2,1,0:T(8,128)(2,1)}, bf16[2,1024,128]{2,1,0:T(8,128)(2,1)S(1)}, u32[]{:S(2)}, u32[]{:S(2)}) collective-permute-start(bf16[2,1024,128]{2,1,0:T(8,128)(2,1)} %slice.5), channel_id=1, source_target_pairs={{0,32},{32,64},{64,96},{96,128},{128,160},{160,192},{192,224},{224... | collective-permute-start | bytes 1572872 | tf_op jit(solution)/shard_map/cond/branch_1_fun/ppermute | solution.py:347
  83.6 21.0 %copy-start.6 = (bf16[1024,128]{1,0:T(8,128)(2,1)S(1)}, bf16[1024,128]{1,0:T(8,128)(2,1)}, u32[]{:S(2)}) copy-start(bf16[1024,128]{1,0:T(8,128)(2,1)} %get-tuple-element.40.grad_ref) | copy-start | bytes 786436 | tf_op jit(solution)/shard_map/cond
  83.6 98.0 %all-to-all-start.3 = ((bf16[16,96,512]{2,1,0:T(8,128)(2,1)}), bf16[16,96,512]{2,1,0:T(8,128)(2,1)}, u32[]{:S(2)}, u32[]{:S(2)}) async-start(bf16[16,96,512]{2,1,0:T(8,128)(2,1)} %cluster.3), calls=%async_computation.3 | async-start | bytes 3145728 | tf_op jit(solution)/shard_map/cond/branch_1_fun/all_to_all | solution.py:353
  110.9 70.6 %collective-permute-start.3 = (bf16[2,1024,128]{2,1,0:T(8,128)(2,1)S(1)}, bf16[2,1024,128]{2,1,0:T(8,128)(2,1)S(1)}, u32[]{:S(2)}, u32[]{:S(2)}) collective-permute-start(bf16[2,1024,128]{2,1,0:T(8,128)(2,1)S(1)} %get-tuple-element.49), channel_id=1, source_target_pairs={{32,0},{64,32},{96,64},{128,96},{160,128},{192,160},{224,192},{256... | collective-permute-start | bytes 1572872 | tf_op jit(solution)/shard_map/cond/branch_1_fun/ppermute | solution.py:347
  185.9 0.9 copy-start.4

commit v6 on v5

--- a/solution.py
+++ b/solution.py
@@ -10,7 +10,7 @@
 EMPTY = 512.0
 masked_fill = -1e30
 LOCAL_FLOPS = 10 * 1024 * 1280 * 128
-HIDDEN_FLOPS = 200 * 10**9
+HIDDEN_FLOPS = 100 * 10**9
 
 
 def dot_nn(a, b):

time: 187 us -> 186 us (level)
  transfers between devices with their start and end apart: 4 -> 4, of which waited for: 2 -> 2; matrix products, arithmetic and copies ran while one was open for 1% -> 1% of each run, Pallas kernels for 7% -> 8%
where the time goes in v6:
time: 186 us
  waiting for transfers between devices  119 us (64%)
  starting transfers between devices  41.4 us (22%)
  Pallas kernels  22 us (12%)
    ppermute x2, waiting for transfers between devices, shifted(): lax.ppermute(block, 'seq', [(i - distance, i) for i in devices if i - dis...  68.4 us
    all_to_all x2, waiting for transfers between devices, exchange(): return lax.all_to_all(block, 'seq', split_axis=0, concat_axis=0, tiled=True)  50.4 us
    all_to_all x2, starting transfers between devices, exchange(): return lax.all_to_all(block, 'seq', split_axis=0, concat_axis=0, tiled=True)  36.2 us
    pallas_call x1, Pallas kernels, cluster_attention(): pl.pallas_call(cluster_kernel, out_shape=jax.ShapeDtypeStruct(received.sh...  7.31 us
    pallas_call x1, Pallas kernels, local_attention(): pl.pallas_call(local_kernel, out_shape=(jax.ShapeDtypeStruct((tokens, hea...  7.2 us
    ppermute x2, starting transfers between devices, shifted(): lax.ppermute(block, 'seq', [(i - distance, i) for i in devices if i - dis...  5.13 us
    pallas_call x1, Pallas kernels, route(): pl.pallas_call(route_kernel, out_shape=(jax.ShapeDtypeStruct((clusters, S...  4.95 us
  transfers between devices with their start and end apart: 4, of which 2 were waited for; matrix products, arithmetic and copies ran while one was open for 1% of the time, Pallas kernels for 8%

profile of v6, /device:TPU:24, one launch (start us, length us, event | category | flops | bytes accessed | tf_op | source)
XLA Modules:
  0.0 185.5 jit_solution(1305572719125301912)
XLA Ops:
  0.6 184.7 %conditional.1 = (bf16[1024,128]{1,0:T(8,128)(2,1)}, bf16[1024,128]{1,0:T(8,128)(2,1)}, bf16[3,1024,128]{2,1,0:T(8,128)(2,1)}, bf16[3,1024,128]{2,1,0:T(8,128)(2,1)}) conditional(s32[]{:T(128)} %convert_element_type.15, (bf16[3,1024,128]{2,1,0:T(8,128)(2,1)}, s32[1,1024]{1,0:T(1,128)}, bf16[3,1024,128]{2,1,0:T(8,128)(2,1)}, ...), branch_computations={%region_0.0_spmd, %region_1.0_spmd} | conditional | flops 100001177600 | bytes 29360448 | solution.py:397
  0.9 5.0 %route.3 = (bf16[16,96,512]{2,1,0:T(8,128)(2,1)}, s32[1024,128]{1,0:T(8,128)S(1)}) custom-call(s32[1,1024]{1,0:T(1,128)} %get-tuple-element.41.labels_hbm, bf16[3,1024,128]{2,1,0:T(8,128)(2,1)} %get-tuple-element.42.qkv_hbm, bf16[1024,128]{1,0:T(8,128)(2,1)} %get-tuple-element.43.grad_hbm), custom_call_target="tpu_custom_call" | custom-call | tf_op jit(solution)/shard_map/cond/branch_1_fun/route/pallas_call | solution.py:121
  5.8 0.0 copy-start.3
  5.8 15.3 %all-to-all-start.2 = ((bf16[16,96,512]{2,1,0:T(8,128)(2,1)}), bf16[16,96,512]{2,1,0:T(8,128)(2,1)S(1)}, u32[]{:S(2)}, u32[]{:S(2)}) async-start(bf16[16,96,512]{2,1,0:T(8,128)(2,1)} %get-tuple-element.44), calls=%async_computation.2 | async-start | bytes 3145728 | tf_op jit(solution)/shard_map/cond/branch_1_fun/all_to_all | solution.py:353
  21.2 0.0 copy-done.3
  21.2 0.8 slice.5
  22.0 3.8 %collective-permute-start.2 = (bf16[2,1024,128]{2,1,0:T(8,128)(2,1)}, bf16[2,1024,128]{2,1,0:T(8,128)(2,1)S(1)}, u32[]{:S(2)}, u32[]{:S(2)}) collective-permute-start(bf16[2,1024,128]{2,1,0:T(8,128)(2,1)} %slice.5), channel_id=1, source_target_pairs={{0,32},{32,64},{64,96},{96,128},{128,160},{160,192},{192,224},{224... | collective-permute-start | bytes 1572872 | tf_op jit(solution)/shard_map/cond/branch_1_fun/ppermute | solution.py:347
  25.9 50.4 %all-to-all-done.2.received_ref = bf16[16,96,512]{2,1,0:T(8,128)(2,1)S(1)} async-done(((bf16[16,96,512]{2,1,0:T(8,128)(2,1)}), bf16[16,96,512]{2,1,0:T(8,128)(2,1)S(1)}, u32[]{:S(2)}, u32[]{:S(2)}) %all-to-all-start.2) | async-done | bytes 1572896 | tf_op jit(solution)/shard_map/cond/branch_1_fun/all_to_all | solution.py:353
  76.3 7.3 %cluster.3 = bf16[16,96,512]{2,1,0:T(8,128)(2,1)} custom-call(bf16[16,96,512]{2,1,0:T(8,128)(2,1)S(1)} %all-to-all-done.2.received_ref), custom_call_target="tpu_custom_call" | custom-call | tf_op jit(solution)/shard_map/cond/branch_1_fun/cluster/pallas_call | solution.py:202
  83.6 20.9 %all-to-all-start.3 = ((bf16[16,96,512]{2,1,0:T(8,128)(2,1)}), bf16[16,96,512]{2,1,0:T(8,128)(2,1)S(1)}, u32[]{:S(2)}, u32[]{:S(2)}) async-start(bf16[16,96,512]{2,1,0:T(8,128)(2,1)} %cluster.3), calls=%async_computation.3 | async-start | bytes 3145728 | tf_op jit(solution)/shard_map/cond/branch_1_fun/all_to_all | solution.py:353
  104.5 0.0 collective-permute-done.2.prev_ref
  104.5 7.2 %local.3 = (bf16[1024,128]{1,0:T(8,128)(2,1)}, bf16[1024,128]{1,0:T(8,128)(2,1)S(1)}, f32[2,1024,128]{2,1,0:T(8,128)S(1)}, bf16[2,1024,128]{2,1,0:T(8,128)(2,1)S(1)}) custom-call(s32[1]{0:T(128)} %bitcast.2.index_ref, bf16[3,1024,128]{2,1,0:T(8,128)(2,1)S(1)} %copy-done.3, bf16[1024,128]{1,0:T(8,128)(2,1)} %get-tuple-element.40.grad_ref, ...), custom_call_target="tpu_custom_call" | custom-call | flops 99999997952 | bytes 1572864 | tf_op jit(solution)/shard_map/cond/branch_1_fun/local/pallas_call | solution.py:322
  111.7 1.3 collective-permute-start.3
  113.0 68.4 %collective-permute-done.3 = bf16[2,1024,128]{2,1,0:T(8,128)(2,1)S(1)} collective-permute-done((bf16[2,1024,128]{2,1,0:T(8,128)(2,1)S(1)}, bf16[2,1024,128]{2,1,0:T(8,128)(2,1)S(1)}, u32[]{:S(2)}, u32[]{:S(2)}) %collective-permute-start.3) | collective-permute-done | bytes 524320 | tf_op jit(solution)/shard_map/cond/branch_1_fun/ppermute | solution.py:347
  181.4 0.1 add_convert_fusion.1
  181.5 0.9 pad_maximum_fusion.1
  182.5 0.0 all-to-all-done.3.returned_ref
  182.5 2.6 %unroute.3 = (bf16[1024,128]{1,0:T(8,128)(2,1)}, bf16[3,1024,128]{2,1,0:T(8,128)(2,1)}) custom-call(bf16[16,96,512]{2,1,0:T(8,128)(2,1)S(1)} %all-to-all-done.3.returned_ref, s32[1024,128]{1,0:T(8,128)S(1)} %get-tuple-element.50.target_ref), custom_call_target="tpu_custom_call" | custom-call | tf_op jit(solution)/shard_map/cond/branch_1_fun/unroute/pallas_call | solution.py:260
Async XLA Ops:
  5.8 15.4 %copy-start.3 = (bf16[3,1024,128]{2,1,0:T(8,128)(2,1)S(1)}, bf16[3,1024,128]{2,1,0:T(8,128)(2,1)}, u32[]{:S(2)}) copy-start(bf16[3,1024,128]{2,1,0:T(8,128)(2,1)} %get-tuple-element.39.qkv_ref) | copy-start | bytes 2359300 | tf_op jit(solution)/shard_map/cond
  5.8 70.5 %all-to-all-start.2 = ((bf16[16,96,512]{2,1,0:T(8,128)(2,1)}), bf16[16,96,512]{2,1,0:T(8,128)(2,1)S(1)}, u32[]{:S(2)}, u32[]{:S(2)}) async-start(bf16[16,96,512]{2,1,0:T(8,128)(2,1)} %get-tuple-element.44), calls=%async_computation.2 | async-start | bytes 3145728 | tf_op jit(solution)/shard_map/cond/branch_1_fun/all_to_all | solution.py:353
  22.0 82.5 %collective-permute-start.2 = (bf16[2,1024,128]{2,1,0:T(8,128)(2,1)}, bf16[2,1024,128]{2,1,0:T(8,128)(2,1)S(1)}, u32[]{:S(2)}, u32[]{:S(2)}) collective-permute-start(bf16[2,1024,128]{2,1,0:T(8,128)(2,1)} %slice.5), channel_id=1, source_target_pairs={{0,32},{32,64},{64,96},{96,128},{128,160},{160,192},{192,224},{224... | collective-permute-start | bytes 1572872 | tf_op jit(solution)/shard_map/cond/branch_1_fun/ppermute | solution.py:347
  83.6 98.8 %all-to-all-start.3 = ((bf16[16,96,512]{2,1,0:T(8,128)(2,1)}), bf16[16,96,512]{2,1,0:T(8,128)(2,1)S(1)}, u32[]{:S(2)}, u32[]{:S(2)}) async-start(bf16[16,96,512]{2,1,0:T(8,128)(2,1)} %cluster.3), calls=%async_computation.3 | async-start | bytes 3145728 | tf_op jit(solution)/shard_map/cond/branch_1_fun/all_to_all | solution.py:353
  111.7 69.6 %collective-permute-start.3 = (bf16[2,1024,128]{2,1,0:T(8,128)(2,1)S(1)}, bf16[2,1024,128]{2,1,0:T(8,128)(2,1)S(1)}, u32[]{:S(2)}, u32[]{:S(2)}) collective-permute-start(bf16[2,1024,128]{2,1,0:T(8,128)(2,1)S(1)} %get-tuple-element.49), channel_id=1, source_target_pairs={{32,0},{64,32},{96,64},{128,96},{160,128},{192,160},{224,192},{256... | collective-permute-start | bytes 1572872 | tf_op jit(solution)/shard_map/cond/branch_1_fun/ppermute | solution.py:347
